TPU v7x, 256 devices: a whole 4x4x8 slice. The times are simulated.
256 devices in a mesh: dp: 4 (over y), outer: 4 (over x_hi, core), inner: 16 (over z, x_lo).
Axes of the slice: x: 4 (x_hi: 2, x_lo: 2; x = x_hi * 2 + x_lo), y: 4, z: 8, core: 2. Of those that a mesh axis runs over, the one named last changes fastest.
Arguments:
- activations: bfloat16 [4, 8192, 4096], P('dp', ('outer', 'inner')), may hold values from -28 to 28
- weights: bfloat16 [4096, 384], P('dp'), may hold values from -0.09375 to 0.09375
- positions: int32 [4, 8192], P('dp', ('outer', 'inner')), may hold values from 0 to 8191, each once within a row
- out_grad: bfloat16 [4, 8192, 128], P('dp', ('outer', 'inner')), may hold values from -6 to 6
Outputs:
- grad_activations: float32 [4, 8192, 4096], P('dp', ('outer', 'inner'))
- grad_weights: float32 [4096, 384], P('dp')
Inputs may be any that keep to these rules, and one draw needn't show every extreme that they name: Each row of positions holds every position of its sequence once.
All inputs are finite; a program needn't handle non-finite values.
Results may differ from a plain program's by a relative error of at most 0.024.
Values may be sent and summed in bfloat16 or wider, within the bound.
A program may use at most 64 MiB of HBM per device.

v0:
```python
import jax
import jax.numpy as jnp
from jax import lax
from jax.sharding import PartitionSpec as P

HEADS = 1
HEAD_DIM = 128


ROPE_BASE = 500000.0
HIGH = lax.Precision.HIGHEST


def rope_tables(places):
    half_dim = HEAD_DIM // 2
    steps_up = jnp.arange(half_dim, dtype=jnp.float32)
    frequency = ROPE_BASE ** (-(steps_up * 2.0 / HEAD_DIM))
    angles = places.astype(jnp.float32)[:, None] * frequency[None, :]
    cosine_rows = jnp.cos(angles)
    sine_rows = jnp.sin(angles)
    return (
        jnp.concatenate([cosine_rows, cosine_rows], 1),
        jnp.concatenate([sine_rows, sine_rows], 1),
    )


def rotate(values, cosine_rows, sine_rows, direction):
    half_dim = values.shape[-1] // 2
    turned = jnp.concatenate([-values[..., half_dim:], values[..., :half_dim]], -1)
    return values * cosine_rows + direction * turned * sine_rows


def shards(activations, weights, positions, out_grad):
    local_activations = activations[0]
    places = positions[0]
    tok_count = local_activations.shape[0]
    width_q = HEADS * HEAD_DIM
    score_scale = HEAD_DIM ** (-0.5)
    full_weights = lax.all_gather(weights, "dp", axis=0, tiled=True)
    projected = jnp.dot(local_activations, full_weights, preferred_element_type=jnp.float32)
    cosine_rows, sine_rows = rope_tables(places)
    queries = projected[:, :width_q].reshape(tok_count, HEADS, HEAD_DIM).transpose(1, 0, 2)
    queries = rotate(queries, cosine_rows, sine_rows, 1.0).astype(jnp.bfloat16)
    keys_own = rotate(projected[:, width_q : width_q + HEAD_DIM], cosine_rows, sine_rows, 1.0)
    key_value = jnp.concatenate([keys_own, projected[:, width_q + HEAD_DIM :]], 1).astype(
        jnp.bfloat16
    )
    grad_heads = out_grad[0].reshape(tok_count, HEADS, HEAD_DIM).transpose(1, 0, 2)

    def scores_of(key_matrix_rows, key_places):
        scores = (
            jnp.einsum(
                "hqd,kd->hqk",
                queries,
                key_matrix_rows[:, :HEAD_DIM],
                preferred_element_type=jnp.float32,
            )
            * score_scale
        )
        visible = places[:, None] >= key_places[None, :]
        return jnp.where(visible[None], scores, -jnp.inf)

    gathered = (
        lax.all_gather(key_value, ("outer", "inner"), axis=0, tiled=True),
        lax.all_gather(places, ("outer", "inner"), axis=0, tiled=True),
    )
    key_matrix_rows, key_places = gathered
    row_max = jnp.full((HEADS, tok_count), -1e30, jnp.float32)
    scores = scores_of(key_matrix_rows, key_places)
    new_max = jnp.maximum(row_max, jnp.max(scores, -1))
    exp_scores = jnp.exp(scores - new_max[..., None])
    row_total = jnp.sum(exp_scores, -1)
    value_rows = key_matrix_rows[:, HEAD_DIM:].astype(jnp.float32)
    weighted = jnp.einsum("hqk,kd->hqd", exp_scores, value_rows, precision=HIGH)
    forward_state = (new_max, row_total, weighted)
    row_max, row_total, weighted = forward_state
    outputs = weighted / row_total[..., None]
    log_total = row_max + jnp.log(row_total)
    delta_rows = jnp.sum(grad_heads.astype(jnp.float32) * outputs, -1)
    key_matrix_rows, key_places = gathered
    scores = scores_of(key_matrix_rows, key_places)
    attn_probs = jnp.exp(scores - log_total[..., None])
    grad_value = jnp.einsum(
        "hqk,hqd->kd",
        attn_probs.astype(jnp.bfloat16),
        grad_heads,
        preferred_element_type=jnp.float32,
    )
    grad_probs = jnp.einsum(
        "hqd,kd->hqk", grad_heads, key_matrix_rows[:, HEAD_DIM:], preferred_element_type=jnp.float32
    )
    grad_scores = (attn_probs * (grad_probs - delta_rows[..., None])).astype(jnp.bfloat16)
    grad_query = jnp.einsum(
        "hqk,kd->hqd",
        grad_scores,
        key_matrix_rows[:, :HEAD_DIM],
        preferred_element_type=jnp.float32,
    )
    grad_key = (
        jnp.einsum("hqk,hqd->kd", grad_scores, queries, preferred_element_type=jnp.float32)
        * score_scale
    )
    key_grads = jnp.concatenate([grad_key, grad_value], 1)
    grad_query, key_grads = (grad_query, key_grads)
    key_sums = lax.psum_scatter(key_grads, ("outer", "inner"), scatter_dimension=0, tiled=True)
    grad_query = rotate(grad_query * score_scale, cosine_rows, sine_rows, -1.0)
    grad_key = rotate(key_sums[:, :HEAD_DIM], cosine_rows, sine_rows, -1.0)
    grad_proj = jnp.concatenate(
        [
            grad_query.transpose(1, 0, 2).reshape(tok_count, width_q),
            grad_key,
            key_sums[:, HEAD_DIM:],
        ],
        1,
    ).astype(jnp.bfloat16)
    grad_acts = lax.dot_general(
        grad_proj, full_weights, (((1,), (1,)), ((), ())), preferred_element_type=jnp.float32
    )
    weight_share = lax.psum_scatter(
        lax.dot_general(
            local_activations,
            grad_proj,
            (((0,), (0,)), ((), ())),
            preferred_element_type=jnp.float32,
        ).astype(jnp.bfloat16),
        "dp",
        scatter_dimension=0,
        tiled=True,
    ).astype(jnp.float32)
    grad_weights = lax.psum(weight_share, ("outer", "inner"))
    return (grad_acts[None], grad_weights)


def solution(mesh):
    placed = (
        P("dp", ("outer", "inner"), None),
        P("dp", None),
        P("dp", ("outer", "inner")),
        P("dp", ("outer", "inner"), None),
    )
    return jax.shard_map(
        shards,
        mesh=mesh,
        in_specs=placed,
        out_specs=(P("dp", ("outer", "inner"), None), P("dp", None)),
        check_vma=False,
    )
```

profile of v0, /device:TPU:1, one launch (start us, length us, event | category | flops | bytes accessed | tf_op | source)
XLA Modules:
  0.0 845.2 jit_solution(472106177290876730)
XLA Ops:
  7.2 0.0 copy-start
  7.2 0.0 copy-start.3
  7.2 0.0 copy-start.2
  7.2 0.0 all-gather.4.cloned.1.call-start
  7.2 0.7 all-gather.4.cloned.1.call-update
  7.9 0.0 all-gather.6.cloned.1.call-start
  8.0 0.7 bitcast_convert_fusion
  8.7 0.3 multiply_cosine_fusion
  9.0 46.6 %all-gather.4.cloned.1.call-done = bf16[4096,384]{1,0:T(8,128)(2,1)} async-done(((bf16[1024,384]{1,0:T(8,128)(2,1)}), bf16[4096,384]{1,0:T(8,128)(2,1)}) %all-gather.4.cloned.1.call-update) | async-done | bytes 3145744 | tf_op jit(solution)/shard_map/all_gather | solution.py:39
  55.5 0.0 copy-done
  55.5 2.6 fusion.33
  58.2 0.1 slice_negate_fusion.2
  58.3 0.1 fusion.40
  58.3 0.1 fusion.39
  58.5 0.6 pad_maximum_fusion.4
  59.1 0.0 all-gather.6.cloned.1.call-update
  59.2 0.0 reduce-scatter.3.cloned.1.call-start
  59.2 0.0 copy-done.2
  59.2 0.1 copy.6
  59.3 0.0 copy-done.3
  59.3 114.6 %all-gather = s32[1,8192]{1,0:T(1,128)S(1)} all-gather(s32[1,128]{1,0:T(1,128)S(1)} %copy-done.3), channel_id=2, replica_groups=mesh['dp'=4,'outer'=4,'inner'=16] {'outer','inner'}, dimensions={1}, use_global_device_ids=true | all-gather | bytes 33280 | tf_op jit(solution)/shard_map/all_gather | solution.py:65
  173.9 71.8 %all-gather.6.cloned.1.call-done = bf16[8192,256]{1,0:T(8,128)(2,1)} async-done(((bf16[128,256]{1,0:T(8,128)(2,1)}), bf16[8192,256]{1,0:T(8,128)(2,1)}) %all-gather.6.cloned.1.call-update) | async-done | bytes 4194320 | tf_op jit(solution)/shard_map/all_gather | solution.py:64
  245.7 2.4 fusion.51
  248.1 0.8 fusion.6
  248.9 0.0 copy-start.1
  248.9 0.9 fusion.8
  249.8 1.3 copy-done.1
  251.1 3.2 fusion.29
  254.3 1.2 fusion.3
  255.5 0.8 convolution_multiply_fusion
  256.2 3.8 pad_maximum_fusion
  260.0 0.0 reduce-scatter.3.cloned.1.call-update
  260.0 0.0 reduce-scatter.5.cloned.1.call-start
  260.1 2.3 fusion.17
  262.4 0.1 fusion.37
  262.5 269.4 %reduce-scatter.3.cloned.1.call-done = f32[128,256]{1,0:T(8,128)} async-done(((f32[8192,256]{1,0:T(8,128)}), f32[128,256]{1,0:T(8,128)}) %reduce-scatter.3.cloned.1.call-update) | async-done | bytes 131088 | tf_op jit(solution)/shard_map/reduce_scatter | solution.py:105
  531.9 0.8 slice.126
  532.8 1.0 slice_negate_fusion
  533.8 1.0 fusion.45
  534.7 2.7 fusion.4
  537.4 0.0 reduce-scatter.5.cloned.1.call-update
  537.4 4.3 convolution_bitcast_fusion
  541.7 42.5 %reduce-scatter.5.cloned.1.call-done = bf16[1024,384]{0,1:T(8,128)(2,1)} async-done(((bf16[4096,384]{0,1:T(8,128)(2,1)}), bf16[1024,384]{0,1:T(8,128)(2,1)}) %reduce-scatter.5.cloned.1.call-update) | async-done | bytes 786448 | tf_op jit(solution)/shard_map/reduce_scatter | solution.py:119
  584.3 252.7 %all-reduce.1 = f32[1024,384]{0,1:T(8,128)S(1)} all-reduce(bf16[1024,384]{0,1:T(8,128)(2,1)} %reduce-scatter.5.cloned.1.call-done), channel_id=1, replica_groups=mesh['dp'=4,'outer'=4,'inner'=16] {'outer','inner'}, use_global_device_ids=true, to_apply=%region_5.6 | all-reduce | flops 393216 | bytes 2359296 | tf_op jit(solution)/shard_map/psum | solution.py:130
  837.0 1.6 copy.11
  (5 shorter events, 0.0 us)
Async XLA Ops:
  7.2 48.4 %copy-start = (bf16[1,128,4096]{2,1,0:T(8,128)(2,1)S(1)}, bf16[1,128,4096]{2,1,0:T(8,128)(2,1)}, u32[]{:S(2)}) copy-start(bf16[1,128,4096]{2,1,0:T(8,128)(2,1)} %param.4) | copy-start | bytes 3145732
  7.2 52.2 %copy-start.3 = (s32[1,128]{1,0:T(1,128)S(1)}, s32[1,128]{1,0:T(1,128)}, u32[]{:S(2)}) copy-start(s32[1,128]{1,0:T(1,128)} %param.6) | copy-start | bytes 1540
  7.2 52.0 %copy-start.2 = (bf16[1,128,128]{2,1,0:T(8,128)(2,1)S(1)}, bf16[1,128,128]{2,1,0:T(8,128)(2,1)}, u32[]{:S(2)}) copy-start(bf16[1,128,128]{2,1,0:T(8,128)(2,1)} %param.7) | copy-start | bytes 98308
  7.2 48.3 %all-gather.4.cloned.1.call-start = ((), (), s32[]{:S(2)}) async-start(), calls=%async_computation.2 | async-start | bytes 3932160 | tf_op jit(solution)/shard_map/all_gather | solution.py:39
  7.9 237.8 %all-gather.6.cloned.1.call-start = ((), (), s32[]{:S(2)}) async-start(), calls=%async_computation.3 | async-start | bytes 4259840 | tf_op jit(solution)/shard_map/all_gather | solution.py:64
  59.2 472.8 %reduce-scatter.3.cloned.1.call-start = ((), (), s32[]{:S(2)}) async-start(), calls=%async_computation.4 | async-start | bytes 8519680 | tf_op jit(solution)/shard_map/reduce_scatter | solution.py:105
  248.9 2.2 copy-start.1
  260.0 324.2 %reduce-scatter.5.cloned.1.call-start = ((), (), s32[]{:S(2)}) async-start(), calls=%async_computation.5 | async-start | bytes 3932160 | tf_op jit(solution)/shard_map/reduce_scatter | solution.py:119
Sparse Core Ops, SparseCore 0:
  9.8 45.6 all-gather.3
  59.3 186.3 all-gather.5
  260.2 271.7 reduce-scatter.2
  537.5 46.6 reduce-scatter.4
where the time goes:
time: 858 us; the launch traced here: 845 us
  waiting for transfers between devices  431 us (50%)
  blocking collectives  367 us (43%)
  matrix products  20.3 us (2%)
  between operations  13.9 us (2%)
    reduce_scatter x1, waiting for transfers between devices, shards(): lax.psum_scatter(key_grads, ('outer', 'inner'), scatter_dimension=0, tile...  269 us
    psum x1, blocking collectives, shards(): grad_weights = lax.psum(weight_share, ('outer', 'inner'))  253 us
    all_gather x1, blocking collectives, shards(): lax.all_gather(places, ('outer', 'inner'), axis=0, tiled=True)  115 us
    all_gather x1, waiting for transfers between devices, shards(): lax.all_gather(key_value, ('outer', 'inner'), axis=0, tiled=True)  71.8 us
    all_gather x1, waiting for transfers between devices, shards(): full_weights = lax.all_gather(weights, 'dp', axis=0, tiled=True)  46.6 us
    reduce_scatter x1, waiting for transfers between devices, shards(): lax.psum_scatter(lax.dot_general(local_activations, grad_proj, (((0,), (0...  42.5 us
  transfers between devices with their start and end apart: 4, of which 4 were waited for; matrix products, arithmetic and copies ran while one was open for 1% of the time, Pallas kernels for 0%

commit v1 on v0

v1 whole, which is shorter than its diff:
```python
import jax
import jax.numpy as jnp
import numpy as np
from jax import lax
from jax.experimental import pallas as pl
from jax.experimental.pallas import tpu as pltpu
from jax.sharding import PartitionSpec as P

HEAD_DIM = 128
ROPE_BASE = 500000.0
NX, NY, NZ, NC = 4, 4, 8, 2
TOK = 128
WIDE = 3 * HEAD_DIM
MESH = pl.DeviceIdType.MESH
BF = jnp.bfloat16
F32 = jnp.float32
SCALE = HEAD_DIM ** (-0.5)
EXP2_SCALE = SCALE * 1.4426950408889634
LOW = -1e30


def coords():
    outer, inner = lax.axis_index("outer"), lax.axis_index("inner")
    return (
        (outer // 2) * 2 + lax.rem(inner, 2),
        lax.axis_index("dp"),
        inner // 2,
        lax.rem(outer, 2),
    )


def device(x, y, z, c):
    return {"dp": y, "outer": (x // 2) * 2 + c, "inner": z * 2 + lax.rem(x, 2)}


def nt(a, b):
    return lax.dot_general(a, b, (((1,), (1,)), ((), ())), preferred_element_type=F32)


def nn(a, b):
    return lax.dot_general(a, b, (((1,), (0,)), ((), ())), preferred_element_type=F32)


def turn(u):
    lane = lax.broadcasted_iota(jnp.int32, u.shape, 1)
    half = jnp.roll(u, HEAD_DIM // 2, 1) if False else pltpu.roll(u, HEAD_DIM // 2, 1)
    return jnp.where(lane < HEAD_DIM // 2, -half, half)


def kernel(
    freq_ref, act_hbm, w_hbm, pos_hbm, og_hbm, ga_hbm, gw_hbm,
    act_v, w_v, og_all, q_all, posq, posk, poskt, kv_all, kt_all, proj,
    e_all, dp_all, ds_all, mb, lb, ab, st_all,
    dq_out, dq_in, dkv_out, dkv_in, gp_all, actx, actxt,
    dwx_out, dwx_in, dwx_own, dwz_out, dwz_in, dw_all, ga_v, gw_v,
    lsem, wsem_s, wsem_r, osem_s, osem_r, psem_s, psem_r, ksem_s, ksem_r,
    qsem_s, qsem_r, kvsem_s, kvsem_r, asem_s, asem_r, ssem_s, ssem_r,
    dqsem_s, dqsem_r, dkvsem_s, dkvsem_r, gsem_s, gsem_r,
    xsem_s, xsem_r, zsem_s, zsem_r, zgsem_s, zgsem_r, xgsem_s, xgsem_r,
):
    x, y, z, c = coords()
    other = 1 - c
    xc, yc = x * 2 + c, y * 2 + c
    sends = []

    def xpeer(k):
        return device(lax.rem(x + k, NX), y, z, c)

    def ypeer(k):
        return device(x, lax.rem(y + k, NY), z, c)

    def zpeer(k):
        return device(x, y, lax.rem(z + k, NZ), c)

    sibling = device(x, y, z, other)

    def send(src, dst, ss, rs, dev):
        cp = pltpu.make_async_remote_copy(src, dst, ss, rs, device_id=dev, device_id_type=MESH)
        cp.start()
        sends.append(cp)

    def arrived(dst, rs):
        pltpu.make_async_remote_copy(
            dst, dst, rs, rs, device_id=sibling, device_id_type=MESH
        ).wait_recv()

    def rows(i, n):
        return pl.ds(pl.multiple_of(i * n, n), n)

    cross = [(k, d) for k in range(4) for d in range(2)][1:]

    lw = pltpu.make_async_copy(w_hbm, w_v.at[rows(y, 1024)], lsem.at[0])
    lw.start()
    lp = pltpu.make_async_copy(pos_hbm, posq.at[z], lsem.at[1])
    lp.start()
    lo = pltpu.make_async_copy(og_hbm.at[0], og_all.at[rows(z, TOK)], lsem.at[2])
    lo.start()
    la = pltpu.make_async_copy(act_hbm.at[0], act_v, lsem.at[3])
    la.start()
    lk = pltpu.make_async_copy(pos_hbm, posk.at[xc], lsem.at[4])
    lk.start()

    barrier = pltpu.get_barrier_semaphore()
    greet = [sibling] + [zpeer(k) for k in range(1, NZ)]
    for k in range(1, 4):
        greet += [xpeer(k), ypeer(k)]
        greet += [
            device(lax.rem(x + k, NX), y, z, other),
            device(x, lax.rem(y + k, NY), z, other),
        ]
    for dev in greet:
        pl.semaphore_signal(barrier, inc=1, device_id=dev, device_id_type=MESH)
    pl.semaphore_wait(barrier, len(greet))

    KVC, QC = pl.ds(HEAD_DIM, 2 * HEAD_DIM), pl.ds(0, HEAD_DIM)

    def wblock(owner, half, cols):
        return w_v.at[pl.ds(pl.multiple_of(owner * 1024 + half * 512, 512), 512), cols]

    lw.wait()
    YORDER = (1, 3, 2)
    for part, cols in enumerate((KVC, QC)):
        for k in YORDER:
            blk = wblock(y, c, cols)
            send(blk, blk, wsem_s.at[part, 0, k], wsem_r.at[part, 0, k], ypeer(k))
    lo.wait()
    lp.wait()
    lk.wait()
    for k in range(1, NZ):
        blk = posq.at[z]
        send(blk, blk, psem_s.at[k], psem_r.at[k], zpeer(k))
    for k, d in cross:
        blk = posk.at[xc]
        dev = device(lax.rem(x + k, NX), y, z, c if d == 0 else other)
        send(blk, blk, ksem_s.at[2 * k + d], ksem_r.at[2 * k + d], dev)
    for k in range(1, NZ):
        blk = og_all.at[rows(z, TOK)]
        send(blk, blk, osem_s.at[k], osem_r.at[k], zpeer(k))

    place = posq[z].astype(F32)
    angles = jnp.broadcast_to(place, (TOK, HEAD_DIM)).T * freq_ref[...]
    cosine, sine = jnp.cos(angles), jnp.sin(angles)

    la.wait()

    def acts(owner):
        return act_v[:, pl.ds(pl.multiple_of(owner * 1024, 1024), 1024)]

    proj[...] = nn(acts(y), w_v[rows(y, 1024), :])
    for part, cols in enumerate((KVC, QC)):
        for k in YORDER:
            owner = lax.rem(y - k + NY, NY)
            blk = wblock(owner, c, cols)
            arrived(blk, wsem_r.at[part, 0, k])
            send(blk, blk, wsem_s.at[part, 1, k], wsem_r.at[part, 1, k], sibling)
        for k in YORDER:
            owner = lax.rem(y - k + NY, NY)
            arrived(wblock(owner, other, cols), wsem_r.at[part, 1, k])
            proj[:, cols] += nn(acts(owner), w_v[rows(owner, 1024), cols])
        if part == 0:
            keys = proj[:, HEAD_DIM : 2 * HEAD_DIM]
            keys = keys * cosine + turn(keys) * sine
            kv_all[xc, :, :HEAD_DIM] = keys.astype(BF)
            kv_all[xc, :, HEAD_DIM:] = proj[:, 2 * HEAD_DIM :].astype(BF)
            for k, d in cross:
                blk = kv_all.at[xc]
                dev = device(lax.rem(x + k, NX), y, z, c if d == 0 else other)
                send(blk, blk, kvsem_s.at[2 * k + d], kvsem_r.at[2 * k + d], dev)
    queries = proj[:, :HEAD_DIM]
    queries = queries * cosine + turn(queries) * sine
    q_all[rows(z, TOK), :] = queries.astype(BF)
    for k in range(1, NZ):
        blk = q_all.at[rows(z, TOK)]
        send(blk, blk, qsem_s.at[k], qsem_r.at[k], zpeer(k))

    for k, d in cross:
        to_y, to_c = lax.rem(y + k, NY), c if d == 0 else other
        src = act_v.at[:, pl.ds(pl.multiple_of(to_y * 1024 + to_c * 512, 512), 512)]
        send(src, actx.at[yc], asem_s.at[2 * k + d], asem_r.at[2 * k + d], device(x, to_y, z, to_c))
    lx = pltpu.make_async_copy(
        act_v.at[:, pl.ds(pl.multiple_of(y * 1024 + c * 512, 512), 512)], actx.at[yc], lsem.at[5]
    )
    lx.start()

    for k in range(1, NZ):
        arrived(posq.at[lax.rem(z - k + NZ, NZ)], psem_r.at[k])
    for k, d in cross:
        kb = lax.rem(x - k + NX, NX) * 2 + (c if d == 0 else other)
        arrived(posk.at[kb], ksem_r.at[2 * k + d])
    for kb in range(8):
        poskt[kb] = jnp.broadcast_to(posk[kb].astype(F32), (TOK, TOK)).T
    for k in range(1, NZ):
        arrived(og_all.at[rows(lax.rem(z - k + NZ, NZ), TOK)], osem_r.at[k])
    for k in range(1, NZ):
        arrived(q_all.at[rows(lax.rem(z - k + NZ, NZ), TOK)], qsem_r.at[k])
    place_q = jnp.concatenate([posq[i].astype(F32) for i in range(NZ)], 1)

    def block_of(k):
        return lax.rem(x - k // 2 + NX, NX) * 2 + lax.rem(c + lax.rem(k, 2), 2)

    def first(k, carry):
        kb = block_of(k)

        @pl.when(k > 0)
        def _():
            arrived(kv_all.at[kb], kvsem_r.at[k])

        key = kv_all[kb, :, :HEAD_DIM]
        value = kv_all[kb, :, HEAD_DIM:]
        kt_all[kb] = key.T
        pk = poskt[kb]
        pk = jnp.concatenate([pk, pk], 1)
        for j in range(4):
            cols = pl.ds(j * 256, 256)
            s = nt(key, q_all[cols, :])
            dp = nt(value, og_all[cols, :])
            s = jnp.where(place_q[:, j * 256 : (j + 1) * 256] >= pk, s, LOW)
            top = jnp.max(s, 0, keepdims=True)
            e = jnp.exp2((s - top) * EXP2_SCALE)
            e_all[kb, :, cols] = e
            dp_all[kb, :, cols] = dp
            mb[pl.ds(kb, 1), cols] = top
            lb[pl.ds(kb, 1), cols] = jnp.sum(e, 0, keepdims=True)
            ab[pl.ds(kb, 1), cols] = jnp.sum(e * dp, 0, keepdims=True)
        return carry

    lax.fori_loop(0, 8, first, 0)
    top = jnp.max(mb[...], 0, keepdims=True)
    fade = jnp.exp2((mb[...] - top) * EXP2_SCALE)
    st_all[z, 0:1, :] = top
    st_all[z, 1:2, :] = jnp.sum(lb[...] * fade, 0, keepdims=True)
    st_all[z, 2:3, :] = jnp.sum(ab[...] * fade, 0, keepdims=True)
    st_all[z, 3:4, :] = jnp.zeros((1, 1024), F32)
    for k in range(1, NZ):
        blk = st_all.at[z]
        send(blk, blk, ssem_s.at[k], ssem_r.at[k], zpeer(k))

    lx.wait()
    for k, d in cross:
        b = lax.rem(y - k + NY, NY) * 2 + (c if d == 0 else other)
        arrived(actx.at[b], asem_r.at[2 * k + d])

    def turn_block(b, carry):
        actxt[:, pl.ds(pl.multiple_of(b * TOK, TOK), TOK)] = actx[b].T
        return carry

    lax.fori_loop(0, 8, turn_block, 0)

    for k in range(1, NZ):
        arrived(st_all.at[lax.rem(z - k + NZ, NZ)], ssem_r.at[k])
    top = st_all[0, 0:1, :]
    for i in range(1, NZ):
        top = jnp.maximum(top, st_all[i, 0:1, :])
    total = jnp.zeros((1, 1024), F32)
    inner = jnp.zeros((1, 1024), F32)
    for i in range(NZ):
        fade = jnp.exp2((st_all[i, 0:1, :] - top) * EXP2_SCALE)
        total += st_all[i, 1:2, :] * fade
        inner += st_all[i, 2:3, :] * fade
    delta = inner / total
    mb[...] = jnp.exp2((mb[...] - top) * EXP2_SCALE) / total

    def second(k, carry):
        kb = block_of(k)
        dv = jnp.zeros((TOK, HEAD_DIM), F32)
        dk = jnp.zeros((TOK, HEAD_DIM), F32)
        for j in range(4):
            cols = pl.ds(j * 256, 256)
            p = e_all[kb, :, cols] * mb[pl.ds(kb, 1), cols]
            ds = (p * (dp_all[kb, :, cols] - delta[:, j * 256 : (j + 1) * 256])).astype(BF)
            ds_all[rows(kb, TOK), cols] = ds
            dv += nn(p.astype(BF), og_all[cols, :])
            dk += nn(ds, q_all[cols, :])
        dkv_out[kb, :, :HEAD_DIM] = (dk * SCALE).astype(BF)
        dkv_out[kb, :, HEAD_DIM:] = dv.astype(BF)

        @pl.when(k > 0)
        def _():
            pltpu.make_async_remote_copy(
                dkv_out.at[kb], dkv_in.at[xc], dkvsem_s.at[k], dkvsem_r.at[k],
                device_id=device(kb // 2, y, z, lax.rem(kb, 2)), device_id_type=MESH,
            ).start()

        return carry

    lax.fori_loop(0, 8, second, 0)
    kt = jnp.concatenate([kt_all[i] for i in range(8)], 1)
    for j in range(4):
        dq = nn(kt, ds_all[:, j * 256 : (j + 1) * 256]) * SCALE
        dq_out[2 * j] = dq[:, :TOK].astype(BF)
        dq_out[2 * j + 1] = dq[:, TOK:].astype(BF)
    for k in range(1, NZ):
        to = lax.rem(z + k, NZ)
        send(dq_out.at[to], dq_in.at[z], dqsem_s.at[k], dqsem_r.at[k], zpeer(k))

    dkv = dkv_out[xc].astype(F32)
    for k in range(1, 8):
        kb = lax.rem(x + k // 2, NX) * 2 + lax.rem(c + lax.rem(k, 2), 2)
        arrived(dkv_in.at[kb], dkvsem_r.at[k])
        dkv += dkv_in[kb].astype(F32)
    dkey = dkv[:, :HEAD_DIM]
    dkey = dkey * cosine - turn(dkey) * sine
    dq = dq_out[z].astype(F32)
    for k in range(1, NZ):
        frm = lax.rem(z - k + NZ, NZ)
        arrived(dq_in.at[frm], dqsem_r.at[k])
        dq += dq_in[frm].astype(F32)
    dq = dq.T
    dq = dq * cosine - turn(dq) * sine
    gp_all[yc, :, :HEAD_DIM] = dq.astype(BF)
    gp_all[yc, :, HEAD_DIM : 2 * HEAD_DIM] = dkey.astype(BF)
    gp_all[yc, :, 2 * HEAD_DIM :] = dkv[:, HEAD_DIM:].astype(BF)

    blk = gp_all.at[yc]
    for k in (2, 1, 3):
        send(blk, blk, gsem_s.at[0, k], gsem_r.at[0, k], ypeer(k))
    send(blk, blk, gsem_s.at[1, 0], gsem_r.at[1, 0], sibling)

    def acts_grad(j, carry):
        cols = pl.ds(pl.multiple_of(j * 512, 512), 512)
        ga_v[:, cols] = nt(gp_all[yc], w_v[cols, :])
        return carry

    lax.fori_loop(0, 8, acts_grad, 0)
    lga = pltpu.make_async_copy(ga_v, ga_hbm.at[0], lsem.at[6])
    lga.start()
    for k in (1, 3, 2):
        blk = gp_all.at[lax.rem(y - k + NY, NY) * 2 + c]
        arrived(blk, gsem_r.at[0, k])
        send(blk, blk, gsem_s.at[1, k], gsem_r.at[1, k], sibling)
    for k in range(4):
        blk = gp_all.at[lax.rem(y - k + NY, NY) * 2 + other]
        arrived(blk, gsem_r.at[1, k])
    gp = gp_all[...].reshape(8 * TOK, WIDE)
    for i in range(NX):
        dw = nn(actxt[i * 128 : (i + 1) * 128, :], gp)
        dwx_out[i] = dw.astype(BF)

    for k in (2, 1, 3):
        to = lax.rem(x + k, NX)
        send(dwx_out.at[to], dwx_in.at[x], xsem_s.at[k], xsem_r.at[k], xpeer(k))
    dw = dwx_out[x].astype(F32)
    for k in (1, 3, 2):
        frm = lax.rem(x - k + NX, NX)
        arrived(dwx_in.at[frm], xsem_r.at[k])
        dw += dwx_in[frm].astype(F32)
    dwz_out[...] = dw.astype(BF).reshape(8, 16, WIDE)
    for k in (4, 3, 5, 2, 6, 1, 7):
        to = lax.rem(z + k, NZ)
        send(dwz_out.at[to], dwz_in.at[z], zsem_s.at[k], zsem_r.at[k], zpeer(k))
    dw = dwz_out[z].astype(F32)
    for k in range(1, NZ):
        frm = lax.rem(z - k + NZ, NZ)
        arrived(dwz_in.at[frm], zsem_r.at[k])
        dw += dwz_in[frm].astype(F32)

    def piece(zz):
        return pl.ds(pl.multiple_of(c * 512 + x * 128 + zz * 16, 16), 16)

    def band(xx, cc):
        return dw_all.at[pl.ds(pl.multiple_of(cc * 512 + xx * 128, 128), 128)]

    dw_all[piece(z), :] = dw.astype(BF)
    for k in (4, 3, 5, 2, 6, 1, 7):
        blk = dw_all.at[piece(z)]
        send(blk, blk, zgsem_s.at[k], zgsem_r.at[k], zpeer(k))
    for k in range(1, NZ):
        arrived(dw_all.at[piece(lax.rem(z - k + NZ, NZ))], zgsem_r.at[k])
    blk = band(x, c)
    for k in (2, 1, 3):
        send(blk, blk, xgsem_s.at[0, k], xgsem_r.at[0, k], xpeer(k))
    send(blk, blk, xgsem_s.at[1, 0], xgsem_r.at[1, 0], sibling)
    for k in (1, 3, 2):
        blk = band(lax.rem(x - k + NX, NX), c)
        arrived(blk, xgsem_r.at[0, k])
        send(blk, blk, xgsem_s.at[1, k], xgsem_r.at[1, k], sibling)
    for k in (0, 1, 3, 2):
        arrived(band(lax.rem(x - k + NX, NX), other), xgsem_r.at[1, k])
    gw_v[...] = dw_all[...].astype(F32)
    lgw = pltpu.make_async_copy(gw_v, gw_hbm, lsem.at[7])
    lgw.start()

    for k in range(1, 8):
        pltpu.make_async_remote_copy(
            dkv_out.at[0], dkv_in.at[0], dkvsem_s.at[k], dkvsem_r.at[k],
            device_id=sibling, device_id_type=MESH,
        ).wait_send()
    for cp in sends:
        cp.wait_send()
    lga.wait()
    lgw.wait()


def shards(activations, weights, positions, out_grad):
    steps = np.arange(HEAD_DIM // 2, dtype=np.float64)
    freq = (ROPE_BASE ** (-(steps * 2.0 / HEAD_DIM))).astype(np.float32)
    freq = jnp.asarray(np.concatenate([freq, freq])[None])
    hbm = pl.BlockSpec(memory_space=pl.ANY)
    dma = pltpu.SemaphoreType.DMA
    V = pltpu.VMEM
    scratch = [
        V((TOK, 4096), BF), V((4096, WIDE), BF), V((1024, HEAD_DIM), BF), V((1024, HEAD_DIM), BF),
        V((NZ, 1, TOK), jnp.int32), V((8, 1, TOK), jnp.int32), V((8, TOK, TOK), F32),
        V((8, TOK, 2 * HEAD_DIM), BF), V((8, HEAD_DIM, TOK), BF), V((TOK, WIDE), F32),
        V((8, TOK, 1024), F32), V((8, TOK, 1024), F32), V((1024, 1024), BF),
        V((8, 1024), F32), V((8, 1024), F32), V((8, 1024), F32), V((NZ, 4, 1024), F32),
        V((NZ, HEAD_DIM, TOK), BF), V((NZ, HEAD_DIM, TOK), BF),
        V((8, TOK, 2 * HEAD_DIM), BF), V((8, TOK, 2 * HEAD_DIM), BF),
        V((8, TOK, WIDE), BF), V((8, TOK, 512), BF), V((512, 1024), BF),
        V((NX, 128, WIDE), BF), V((NX, 128, WIDE), BF), V((8, 128), F32),
        V((NZ, 16, WIDE), BF), V((NZ, 16, WIDE), BF), V((1024, WIDE), BF),
        V((TOK, 4096), F32), V((1024, WIDE), F32),
        dma((8,)), dma((2, 2, 4)), dma((2, 2, 4)), dma((8,)), dma((8,)), dma((8,)), dma((8,)),
        dma((8,)), dma((8,)), dma((8,)), dma((8,)), dma((8,)), dma((8,)), dma((8,)), dma((8,)),
        dma((8,)), dma((8,)), dma((8,)), dma((8,)), dma((8,)), dma((8,)), dma((2, 4)), dma((2, 4)),
        dma((4,)), dma((4,)), dma((8,)), dma((8,)), dma((8,)), dma((8,)), dma((2, 4)), dma((2, 4)),
    ]
    return tuple(
        pl.pallas_call(
            kernel,
            out_shape=(
                jax.ShapeDtypeStruct((1, TOK, 4096), F32),
                jax.ShapeDtypeStruct((1024, WIDE), F32),
            ),
            in_specs=[pl.BlockSpec(memory_space=pltpu.VMEM)] + [hbm] * 4,
            out_specs=(hbm, hbm),
            scratch_shapes=scratch,
            compiler_params=pltpu.CompilerParams(
                collective_id=0, has_side_effects=True, vmem_limit_bytes=56 << 20
            ),
        )(freq, activations, weights, positions, out_grad)
    )


def solution(mesh):
    placed = (
        P("dp", ("outer", "inner"), None),
        P("dp", None),
        P("dp", ("outer", "inner")),
        P("dp", ("outer", "inner"), None),
    )
    return jax.shard_map(
        shards,
        mesh=mesh,
        in_specs=placed,
        out_specs=(P("dp", ("outer", "inner"), None), P("dp", None)),
        check_vma=False,
    )
```

time: 858 us -> 100 us (0.12); the launches traced: 845 us -> 100 us
  waiting for transfers between devices: 431 us -> 0 us
  blocking collectives: 367 us -> 0 us
  Pallas kernels: 0 us -> 95 us
  matrix products: 20.3 us -> 0 us
  between operations: 13.9 us -> 0.65 us
    reduce_scatter x2 -> x0, waiting for transfers between devices: 312 us -> none  [the longest x1 269 us: shards(): lax.psum_scatter(key_grads, ('outer', 'inner'), scatter_dimension=0, tile...]
    psum x1 -> x0, blocking collectives: 253 us -> none  [shards(): grad_weights = lax.psum(weight_share, ('outer', 'inner'))]
    all_gather x2 -> x0, waiting for transfers between devices: 118 us -> none  [the longest x1 71.8 us: shards(): lax.all_gather(key_value, ('outer', 'inner'), axis=0, tiled=True)]
    all_gather x1 -> x0, blocking collectives: 115 us -> none  [shards(): lax.all_gather(places, ('outer', 'inner'), axis=0, tiled=True)]
    pallas_call x0 -> x1, Pallas kernels: none -> 95 us  [shards(): pl.pallas_call(kernel, out_shape=(jax.ShapeDtypeStruct((1, TOK, 4096), F3...]
    dot_general x9 -> x0, matrix products: 20.3 us -> none  [the longest x1 4.32 us: shards(): lax.dot_general(grad_proj, full_weights, (((1,), (1,)), ((), ())), prefer...]
  transfers between devices with their start and end apart: 4 -> 0, of which waited for: 4 -> 0; matrix products, arithmetic and copies ran while one was open for 1% -> 0% of each run, Pallas kernels for 0% -> 0%
where the time goes in v1:
time: 100 us
  Pallas kernels  95 us (95%)
  local copies, waits for them, and re-layouts  4.38 us (4%)
    pallas_call x1, Pallas kernels, shards(): pl.pallas_call(kernel, out_shape=(jax.ShapeDtypeStruct((1, TOK, 4096), F3...  95 us
    unnamed x4, local copies, waits for them, and re-layouts  4.38 us

profile of v1, /device:TPU:1, one launch (start us, length us, event | category | flops | bytes accessed | tf_op | source)
XLA Modules:
  0.0 100.0 jit_solution(6732291220596269738)
XLA Ops:
  0.6 95.0 %shard_map.68 = (f32[1,128,4096]{2,1,0:T(8,128)}, f32[1024,384]{1,0:T(8,128)}) custom-call(f32[1,128]{1,0:T(1,128)} %constant.2.clone.freq_ref, bf16[1,128,4096]{2,1,0:T(8,128)(2,1)} %act_hbm.1, bf16[1024,384]{1,0:T(8,128)(2,1)} %w_hbm.1, s32[1,128]{1,0:T(1,128)} %pos_hbm.1, bf16[1,128,128]{2,1,0:T(8,128)(2,1)} %og_hbm.1), custom_call_target="tpu_custom_call" | custom-call | tf_op jit(solution)/shard_map/pallas_call | solution.py:419
  95.6 0.0 copy-start
  95.7 3.2 %copy.9 = f32[1,128,4096]{2,1,0:T(8,128)} copy(f32[1,128,4096]{2,1,0:T(8,128)} %get-tuple-element.4) | data formatting | bytes 4194304
  98.9 0.0 copy-done
  98.9 1.1 %copy.10 = f32[1024,384]{1,0:T(8,128)} copy(f32[1024,384]{1,0:T(8,128)S(1)} %copy-done) | data formatting | bytes 3145728
Async XLA Ops:
  95.6 3.2 %copy-start = (f32[1024,384]{1,0:T(8,128)S(1)}, f32[1024,384]{1,0:T(8,128)}, u32[]{:S(2)}) copy-start(f32[1024,384]{1,0:T(8,128)} %get-tuple-element.5) | copy-start | bytes 4718596

commit v2 on v1

v2 whole, which is shorter than its diff:
```python
import jax
import jax.numpy as jnp
import numpy as np
from jax import lax
from jax.experimental import pallas as pl
from jax.experimental.pallas import tpu as pltpu
from jax.sharding import PartitionSpec as P

HEAD_DIM = 128
ROPE_BASE = 500000.0
NX, NY, NZ, NC = 4, 4, 8, 2
TOK = 128
WIDE = 3 * HEAD_DIM
MESH = pl.DeviceIdType.MESH
BF = jnp.bfloat16
F32 = jnp.float32
SCALE = HEAD_DIM ** (-0.5)
EXP2_SCALE = SCALE * 1.4426950408889634
LOW = -1e30
STEPS = ((0, 0), (0, 1), (1, 0), (3, 0), (2, 0), (1, 1), (3, 1), (2, 1))


def coords():
    outer, inner = lax.axis_index("outer"), lax.axis_index("inner")
    return (
        (outer // 2) * 2 + lax.rem(inner, 2),
        lax.axis_index("dp"),
        inner // 2,
        lax.rem(outer, 2),
    )


def device(x, y, z, c):
    return {"dp": y, "outer": (x // 2) * 2 + c, "inner": z * 2 + lax.rem(x, 2)}


def nt(a, b):
    return lax.dot_general(a, b, (((1,), (1,)), ((), ())), preferred_element_type=F32)


def nn(a, b):
    return lax.dot_general(a, b, (((1,), (0,)), ((), ())), preferred_element_type=F32)


def turn(u):
    lane = lax.broadcasted_iota(jnp.int32, u.shape, 1)
    half = jnp.roll(u, HEAD_DIM // 2, 1) if False else pltpu.roll(u, HEAD_DIM // 2, 1)
    return jnp.where(lane < HEAD_DIM // 2, -half, half)


def kernel(
    freq_hbm, act_hbm, w_hbm, pos_hbm, og_hbm, ga_ref, gw_ref,
    freq_v, act_v, w_v, og_all, q_all, posq, posk, poskt, kv_all, kt_all, proj,
    e_all, dp_all, ds_all, mb, lb, ab, dl, acc, p_all, st_all,
    dq_out, dq_in, dkv_out, dkv_in, gp_all, actx, actxt,
    dwx_out, dwx_in, mark, dwz_out, dwz_in, dw_all,
    sent, lsem, wsem_y, wsem_x, wsem_c, psem, ksem, osem, qsem, kvsem_x, kvsem_c, asem, ssem,
    dqsem, dkvsem, gsem_y, gsem_c, xsem, zsem, zgsem, xgsem, sgsem,
):
    x, y, z, c = coords()
    other = 1 - c
    xc, yc = x * 2 + c, y * 2 + c
    sends = []

    def xpeer(k):
        return device(lax.rem(x + k, NX), y, z, c)

    def ypeer(k):
        return device(x, lax.rem(y + k, NY), z, c)

    def zpeer(k):
        return device(x, y, lax.rem(z + k, NZ), c)

    sibling = device(x, y, z, other)

    def send(src, dst, rs, dev):
        cp = pltpu.make_async_remote_copy(src, dst, sent, rs, device_id=dev, device_id_type=MESH)
        cp.start()
        sends.append(cp)

    def arrived(dst, rs):
        pltpu.make_async_remote_copy(
            dst, dst, rs, rs, device_id=sibling, device_id_type=MESH
        ).wait_recv()

    def rows(i, n):
        return pl.ds(pl.multiple_of(i * n, n), n)

    cross = [(k, d) for k in range(4) for d in range(2)][1:]

    lw = pltpu.make_async_copy(w_hbm, w_v.at[rows(y, 1024)], lsem.at[0])
    lw.start()
    lp = pltpu.make_async_copy(pos_hbm, posq.at[z], lsem.at[1])
    lp.start()
    lo = pltpu.make_async_copy(og_hbm.at[0], og_all.at[rows(z, TOK)], lsem.at[1])
    lo.start()
    la = pltpu.make_async_copy(act_hbm.at[0], act_v, lsem.at[2])
    la.start()
    lk = pltpu.make_async_copy(pos_hbm, posk.at[xc], lsem.at[1])
    lk.start()
    lf = pltpu.make_async_copy(freq_hbm, freq_v, lsem.at[1])
    lf.start()

    barrier = pltpu.get_barrier_semaphore()
    greet = [sibling] + [zpeer(k) for k in range(1, NZ)]
    for k in range(1, 4):
        greet += [xpeer(k), ypeer(k)]
        greet += [
            device(lax.rem(x + k, NX), y, z, other),
            device(x, lax.rem(y + k, NY), z, other),
        ]
    for dev in greet:
        pl.semaphore_signal(barrier, inc=1, device_id=dev, device_id_type=MESH)
    pl.semaphore_wait(barrier, len(greet))

    KVC, QC = pl.ds(HEAD_DIM, 2 * HEAD_DIM), pl.ds(0, HEAD_DIM)
    COLS = (QC, KVC)
    YORDER = (1, 3, 2)
    odd = lax.rem(x, 2)
    near, far = odd * 2 + c, (1 - odd) * 2 + c
    near_sib, far_sib = odd * 2 + other, (1 - odd) * 2 + other

    def wblock(owner, piece, cols, start=0, n=256):
        first_row = pl.multiple_of(owner * 1024 + piece * 256 + start, n)
        return w_v.at[pl.ds(first_row, n), cols]

    def wshare(part, k):
        owner, cols = lax.rem(y - k + NY, NY), COLS[part]
        blk = wblock(owner, near, cols)
        arrived(blk, wsem_y.at[part, k])
        if part == 1 and k != 2:
            half = wblock(owner, near, cols, 0 if k == 1 else 128, 128)
            send(half, half, wsem_y.at[part, 2], ypeer(k))
        for i, d in enumerate((1, 3)):
            half = wblock(owner, near, cols, i * 128, 128)
            send(half, half, wsem_x.at[part, k], xpeer(d))
        send(blk, blk, wsem_c.at[part, k], sibling)

    def wpass(part, k):
        owner, cols = lax.rem(y - k + NY, NY), COLS[part]
        blk = wblock(owner, far, cols)
        arrived(blk, wsem_x.at[part, k])
        send(blk, blk, wsem_c.at[part, k], sibling)

    def wuse(part, k):
        owner, cols = lax.rem(y - k + NY, NY), COLS[part]
        arrived(w_v.at[pl.ds(0, 512), cols], wsem_c.at[part, k])
        proj[:, cols] += nn(acts(owner), w_v[rows(owner, 1024), cols])

    lw.wait()
    for part in range(2):
        for k in (1, 3) if part else YORDER:
            blk = wblock(y, near, COLS[part])
            send(blk, blk, wsem_y.at[part, k], ypeer(k))
    lo.wait()
    lp.wait()
    lk.wait()
    lf.wait()
    for k in range(1, NZ):
        blk = posq.at[z]
        send(blk, blk, psem, zpeer(k))
    for k, d in cross:
        blk = posk.at[xc]
        dev = device(lax.rem(x + k, NX), y, z, c if d == 0 else other)
        send(blk, blk, ksem, dev)
    for k in range(1, NZ):
        blk = og_all.at[rows(z, TOK)]
        send(blk, blk, osem, zpeer(k))

    place = posq[z].astype(F32)
    angles = jnp.broadcast_to(place, (TOK, HEAD_DIM)).T * freq_v[...]
    cosine, sine = jnp.cos(angles), jnp.sin(angles)

    la.wait()

    def acts(owner):
        return act_v[:, pl.ds(pl.multiple_of(owner * 1024, 1024), 1024)]

    proj[...] = nn(acts(y), w_v[rows(y, 1024), :])
    for k in YORDER:
        wshare(0, k)
    wshare(1, 1)
    wshare(1, 3)
    for k in YORDER:
        wpass(0, k)
    for k in YORDER:
        wuse(0, k)
    queries = proj[:, :HEAD_DIM]
    queries = queries * cosine + turn(queries) * sine
    q_all[rows(z, TOK), :] = queries.astype(BF)
    for k in range(1, NZ):
        blk = q_all.at[rows(z, TOK)]
        send(blk, blk, qsem, zpeer(k))
    wshare(1, 2)
    wpass(1, 1)
    wpass(1, 3)
    wuse(1, 1)
    wuse(1, 3)
    wpass(1, 2)
    wuse(1, 2)
    keys = proj[:, HEAD_DIM : 2 * HEAD_DIM]
    keys = keys * cosine + turn(keys) * sine
    kv_all[xc, :, :HEAD_DIM] = keys.astype(BF)
    kv_all[xc, :, HEAD_DIM:] = proj[:, 2 * HEAD_DIM :].astype(BF)
    blk = kv_all.at[xc]
    for k in (2, 1, 3):
        send(blk, blk, kvsem_x.at[k], xpeer(k))
    send(blk, blk, kvsem_c.at[0], sibling)

    for k, d in cross:
        to_y, to_c = lax.rem(y + k, NY), c if d == 0 else other
        src = act_v.at[:, pl.ds(pl.multiple_of(to_y * 1024 + to_c * 512, 512), 512)]
        send(src, actx.at[yc], asem, device(x, to_y, z, to_c))
    lx = pltpu.make_async_copy(
        act_v.at[:, pl.ds(pl.multiple_of(y * 1024 + c * 512, 512), 512)], actx.at[yc], lsem.at[3]
    )
    lx.start()

    arrived(posq.at[pl.ds(0, 7)], psem)
    arrived(posk.at[pl.ds(0, 7)], ksem)
    for kb in range(8):
        poskt[kb] = jnp.broadcast_to(posk[kb].astype(F32), (TOK, TOK)).T
    arrived(og_all.at[pl.ds(0, 7 * TOK)], osem)
    arrived(q_all.at[pl.ds(0, 7 * TOK)], qsem)
    place_q = jnp.concatenate([posq[i].astype(F32) for i in range(NZ)], 1)

    def step_of(j):
        i = lax.rem(j + 1, 3)
        dx = jnp.where(j < 2, 0, lax.rem(1 + 2 * i, 4) + i // 2)
        return dx, jnp.where(j < 2, j, (j - 2) // 3)

    def block_of(j):
        dx, dc = step_of(j)
        return lax.rem(x - dx + NX, NX) * 2 + lax.rem(c + dc, 2)

    def relay(k):
        blk = kv_all.at[lax.rem(x - k + NX, NX) * 2 + c]
        arrived(blk, kvsem_x.at[k])
        send(blk, blk, kvsem_c.at[k], sibling)

    def first(k, carry, half):
        kb = block_of(k)
        dx, dc = step_of(k)
        key = kv_all.at[kb, :, pl.ds(0, HEAD_DIM)]
        value = kv_all.at[kb, :, pl.ds(HEAD_DIM, HEAD_DIM)]
        if half == 0:

            @pl.when(dc > 0)
            def _():
                arrived(kv_all.at[kb], kvsem_c.at[dx])

            kt_all[kb] = key[...].T
        pk = poskt[kb]
        pk = jnp.concatenate([pk, pk], 1)
        for j in (2 * half, 2 * half + 1):
            cols = pl.ds(j * 256, 256)
            s = nt(key[...], q_all[cols, :])
            dp = nt(value[...], og_all[cols, :])
            s = jnp.where(place_q[:, j * 256 : (j + 1) * 256] >= pk, s, LOW)
            top = jnp.max(s, 0, keepdims=True)
            e = jnp.exp2((s - top) * EXP2_SCALE)
            e_all[kb, :, cols] = e
            dp_all[kb, :, cols] = dp
            mb[pl.ds(kb, 1), cols] = top
            lb[pl.ds(kb, 1), cols] = jnp.sum(e, 0, keepdims=True)
            ab[pl.ds(kb, 1), cols] = jnp.sum(e * dp, 0, keepdims=True)
        return carry

    def first_half(k, carry):
        return first(k, carry, 0)

    def other_half(k, carry):
        return first(k, carry, 1)

    def stats_send(half):
        cols = pl.ds(half * 512, 512)
        high = mb[:, cols]
        top = jnp.max(high, 0, keepdims=True)
        fade = jnp.exp2((high - top) * EXP2_SCALE)
        total = jnp.sum(lb[:, cols] * fade, 0, keepdims=True)
        st_all[half, z, 0:1, :] = top * EXP2_SCALE + jnp.log2(total)
        st_all[half, z, 1:2, :] = jnp.sum(ab[:, cols] * fade, 0, keepdims=True) / total
        blk = st_all.at[half, z]
        for k in range(1, NZ):
            send(blk, blk, ssem.at[half], zpeer(k))

    def stats_merge(half):
        cols = pl.ds(half * 512, 512)
        arrived(st_all.at[half, pl.ds(0, 7)], ssem.at[half])
        top = st_all[half, 0, 0:1, :]
        for i in range(1, NZ):
            top = jnp.maximum(top, st_all[half, i, 0:1, :])
        total = jnp.zeros((1, 512), F32)
        delta = jnp.zeros((1, 512), F32)
        for i in range(NZ):
            fade = jnp.exp2(st_all[half, i, 0:1, :] - top)
            total += fade
            delta += st_all[half, i, 1:2, :] * fade
        dl[:, cols] = delta / total
        mb[:, cols] = jnp.exp2(mb[:, cols] * EXP2_SCALE - (top + jnp.log2(total)))

    def grads_of(kb, j):
        cols = pl.ds(j * 256, 256)
        p = e_all[kb, :, cols] * mb[pl.ds(kb, 1), cols]
        ds = (p * (dp_all[kb, :, cols] - dl[:, cols])).astype(BF)
        ds_all[rows(kb, TOK), cols] = ds
        return p.astype(BF), ds

    def dq_send(half):
        kt = jnp.concatenate([kt_all[i] for i in range(8)], 1)
        for j in (2 * half, 2 * half + 1):
            dq = nn(kt, ds_all[:, j * 256 : (j + 1) * 256]) * SCALE
            dq_out[2 * j] = dq[:, :TOK].astype(BF)
            dq_out[2 * j + 1] = dq[:, TOK:].astype(BF)
        for to in range(4 * half, 4 * half + 4):

            @pl.when(z != to)
            def _():
                pltpu.make_async_remote_copy(
                    dq_out.at[to], dq_in.at[z], sent, dqsem,
                    device_id=device(x, y, to, c), device_id_type=MESH,
                ).start()

    lax.fori_loop(0, 2, first_half, 0, unroll=True)
    relay(1)
    relay(3)
    lax.fori_loop(2, 4, first_half, 0, unroll=True)
    relay(2)
    lax.fori_loop(4, 8, first_half, 0, unroll=True)
    stats_send(0)
    lax.fori_loop(0, 8, other_half, 0, unroll=True)
    stats_send(1)
    stats_merge(0)

    def second_half0(k, carry):
        dv = jnp.zeros((TOK, HEAD_DIM), F32)
        dk = jnp.zeros((TOK, HEAD_DIM), F32)
        for j in range(2):
            cols = pl.ds(j * 256, 256)
            p, ds = grads_of(k, j)
            dv += nn(p, og_all[cols, :])
            dk += nn(ds, q_all[cols, :])
        acc[k, :, :HEAD_DIM] = dk
        acc[k, :, HEAD_DIM:] = dv
        return carry

    lax.fori_loop(0, 8, second_half0, 0, unroll=True)
    dq_send(0)
    stats_merge(1)

    def second_half1(k, carry):
        for j in range(2, 4):
            p, ds = grads_of(k, j)
            p_all[k, :, pl.ds((j - 2) * 256, 256)] = p
        return carry

    lax.fori_loop(0, 8, second_half1, 0, unroll=True)
    dq_send(1)

    def key_grads(i, carry):
        k = 7 - i
        kb = block_of(k)
        dk = acc[kb, :, :HEAD_DIM] + nn(ds_all[rows(kb, TOK), 512:], q_all[512:, :])
        dv = acc[kb, :, HEAD_DIM:] + nn(p_all[kb], og_all[512:, :])
        dkv_out[kb, :, :HEAD_DIM] = (dk * SCALE).astype(BF)
        dkv_out[kb, :, HEAD_DIM:] = dv.astype(BF)

        @pl.when(k > 0)
        def _():
            pltpu.make_async_remote_copy(
                dkv_out.at[kb], dkv_in.at[xc], sent, dkvsem,
                device_id=device(kb // 2, y, z, lax.rem(kb, 2)), device_id_type=MESH,
            ).start()

        return carry

    lax.fori_loop(0, 8, key_grads, 0, unroll=True)
    lx.wait()
    arrived(actx.at[pl.ds(0, 7)], asem)

    def turn_block(b, carry):
        actxt[:, pl.ds(pl.multiple_of(b * TOK, TOK), TOK)] = actx[b].T
        return carry

    lax.fori_loop(0, 8, turn_block, 0)
    arrived(dkv_in.at[pl.ds(0, 7)], dkvsem)
    dkv = dkv_out[xc].astype(F32)
    for k in range(1, 8):
        dkv += dkv_in[lax.rem(xc + k, 8)].astype(F32)
    dkey = dkv[:, :HEAD_DIM]
    dkey = dkey * cosine - turn(dkey) * sine
    gp_all[yc, :, HEAD_DIM : 2 * HEAD_DIM] = dkey.astype(BF)
    gp_all[yc, :, 2 * HEAD_DIM :] = dkv[:, HEAD_DIM:].astype(BF)

    def third(i):
        return pl.ds(i * HEAD_DIM, HEAD_DIM)

    def gp_send(i):
        blk = gp_all.at[yc, :, third(i)]
        for k in (2, 1, 3):
            send(blk, blk, gsem_y.at[i, k], ypeer(k))
        send(blk, blk, gsem_c.at[i], sibling)

    def gp_relay(i):
        for k in YORDER:
            blk = gp_all.at[lax.rem(y - k + NY, NY) * 2 + c, :, third(i)]
            arrived(blk, gsem_y.at[i, k])
            send(blk, blk, gsem_c.at[i], sibling)

    def dw_send(i):
        arrived(gp_all.at[pl.ds(0, 4), :, third(i)], gsem_c.at[i])
        gp = gp_all[:, :, third(i)].reshape(8 * TOK, HEAD_DIM)
        for j in range(NX):
            dwx_out[i, j] = nn(actxt[j * 128 : (j + 1) * 128, :], gp).astype(BF)
        for k in (2, 1, 3):
            to = lax.rem(x + k, NX)
            send(dwx_out.at[i, to], dwx_in.at[i, x], xsem.at[i], xpeer(k))

    def band_send(i):
        arrived(dwx_in.at[i, pl.ds(0, 3)], xsem.at[i])
        dw = dwx_out[i, x].astype(F32)
        for k in range(1, NX):
            dw += dwx_in[i, lax.rem(x + k, NX)].astype(F32)
        dwz_out[i] = dw.astype(BF).reshape(8, 16, HEAD_DIM)
        for k in (4, 3, 5, 2, 6, 1, 7):
            to = lax.rem(z + k, NZ)
            send(dwz_out.at[i, to], dwz_in.at[i, z], zsem.at[i], zpeer(k))

    def band(i, xx, cc):
        return dw_all.at[i, pl.ds(pl.multiple_of(cc * 512 + xx * 128, 128), 128)]

    def piece_send(i):
        arrived(dwz_in.at[i, pl.ds(0, 7)], zsem.at[i])
        dw = dwz_out[i, z].astype(F32)
        for k in range(1, NZ):
            dw += dwz_in[i, lax.rem(z + k, NZ)].astype(F32)
        own = pl.ds(pl.multiple_of(c * 512 + x * 128 + z * 16, 16), 16)
        dw_all[i, own, :] = dw.astype(BF)
        blk = dw_all.at[i, own]
        for k in (4, 3, 5, 2, 6, 1, 7):
            send(blk, blk, zgsem.at[i], zpeer(k))

    def spread(i):
        arrived(dw_all.at[i, pl.ds(0, 7 * 16)], zgsem.at[i])
        blk = band(i, x, c)
        for k in (2, 1, 3):
            send(blk, blk, xgsem.at[i, k], xpeer(k))
        send(blk, blk, sgsem.at[i], sibling)

    def spread_relay(i):
        for k in (1, 3, 2):
            blk = band(i, lax.rem(x - k + NX, NX), c)
            arrived(blk, xgsem.at[i, k])
            send(blk, blk, sgsem.at[i], sibling)

    def finish(i):
        arrived(dw_all.at[i, pl.ds(0, 512)], sgsem.at[i])
        gw_ref[:, third(i)] = dw_all[i].astype(F32)

    gp_send(2)
    gp_send(1)
    arrived(dq_in.at[pl.ds(0, 7)], dqsem)
    dq = dq_out[z].astype(F32)
    for k in range(1, NZ):
        dq += dq_in[lax.rem(z + k, NZ)].astype(F32)
    dq = dq.T
    dq = dq * cosine - turn(dq) * sine
    gp_all[yc, :, :HEAD_DIM] = dq.astype(BF)
    gp_send(0)

    def acts_grad(j, carry):
        cols = pl.ds(pl.multiple_of(j * 512, 512), 512)
        ga_ref[0, :, cols] = nt(gp_all[yc], w_v[cols, :])
        return carry

    lax.fori_loop(0, 8, acts_grad, 0)
    gp_relay(2)
    dw_send(2)
    gp_relay(1)
    dw_send(1)
    gp_relay(0)
    dw_send(0)
    band_send(2)
    band_send(1)
    band_send(0)
    piece_send(2)
    piece_send(1)
    piece_send(0)
    spread(2)
    spread(1)
    spread(0)
    spread_relay(2)
    spread_relay(1)
    finish(2)
    spread_relay(0)
    finish(1)
    finish(0)

    for out, sem in ((dkv_out, dkvsem), (dq_out, dqsem)):
        blk = out.at[pl.ds(0, 7)]
        pltpu.make_async_remote_copy(
            blk, blk, sent, sem, device_id=sibling, device_id_type=MESH
        ).wait_send()
    for cp in sends:
        cp.wait_send()


def put(ga_ref, gw_ref, ga_hbm, gw_hbm, sem):
    copies = []
    for i in range(2):
        part = pl.ds(i * 64, 64)
        copies.append(pltpu.make_async_copy(ga_ref.at[0, part], ga_hbm.at[0, part], sem.at[0, i]))
        part = pl.ds(i * 512, 512)
        copies.append(pltpu.make_async_copy(gw_ref.at[part], gw_hbm.at[part], sem.at[1, i]))
    for cp in copies:
        cp.start()
    for cp in copies:
        cp.wait()


def shards(activations, weights, positions, out_grad):
    steps = np.arange(HEAD_DIM // 2, dtype=np.float64)
    freq = (ROPE_BASE ** (-(steps * 2.0 / HEAD_DIM))).astype(np.float32)
    freq = jnp.asarray(np.concatenate([freq, freq])[None])
    operands = (freq, activations, weights, positions, out_grad)
    hbm = pl.BlockSpec(memory_space=pltpu.HBM)
    vmem = pl.BlockSpec(memory_space=pltpu.VMEM)
    dma = pltpu.SemaphoreType.DMA
    V = pltpu.VMEM
    scratch = [
        V((1, HEAD_DIM), F32), V((TOK, 4096), BF), V((4096, WIDE), BF), V((1024, HEAD_DIM), BF), V((1024, HEAD_DIM), BF),
        V((NZ, 1, TOK), jnp.int32), V((8, 1, TOK), jnp.int32), V((8, TOK, TOK), F32),
        V((8, TOK, 2 * HEAD_DIM), BF), V((8, HEAD_DIM, TOK), BF), V((TOK, WIDE), F32),
        V((8, TOK, 1024), F32), V((8, TOK, 1024), F32), V((1024, 1024), BF),
        V((8, 1024), F32), V((8, 1024), F32), V((8, 1024), F32), V((1, 1024), F32),
        V((8, TOK, 2 * HEAD_DIM), F32), V((8, TOK, 512), BF), V((2, NZ, 2, 512), F32),
        V((NZ, HEAD_DIM, TOK), BF), V((NZ, HEAD_DIM, TOK), BF),
        V((8, TOK, 2 * HEAD_DIM), BF), V((8, TOK, 2 * HEAD_DIM), BF),
        V((8, TOK, WIDE), BF), V((8, TOK, 512), BF), V((512, 1024), BF),
        V((3, NX, 128, 128), BF), V((3, NX, 128, 128), BF), V((8, 128), F32),
        V((3, NZ, 16, 128), BF), V((3, NZ, 16, 128), BF), V((3, 1024, 128), BF),
        dma(()), dma((4,)), dma((2, 4)), dma((2, 4)), dma((2, 4)), dma(()), dma(()), dma(()), dma(()),
        dma((4,)), dma((4,)), dma(()), dma((2,)), dma(()), dma(()), dma((3, 4)), dma((3,)), dma((3,)),
        dma((3,)), dma((3,)), dma((3, 4)), dma((3,)),
    ]
    grads = pl.pallas_call(
        kernel,
        out_shape=(pltpu.VMEM((1, TOK, 4096), F32), pltpu.VMEM((1024, WIDE), F32)),
        in_specs=[hbm] * 5,
        out_specs=(vmem, vmem),
        scratch_shapes=scratch,
        compiler_params=pltpu.CompilerParams(
            collective_id=0, has_side_effects=True, vmem_limit_bytes=40 << 20
        ),
    )(*(pltpu.with_memory_space_constraint(a, pltpu.HBM) for a in operands))
    return pl.pallas_call(
        put,
        out_shape=(
            jax.ShapeDtypeStruct((1, TOK, 4096), F32),
            jax.ShapeDtypeStruct((1024, WIDE), F32),
        ),
        in_specs=[vmem, vmem],
        out_specs=(hbm, hbm),
        scratch_shapes=[dma((2, 2))],
        compiler_params=pltpu.CompilerParams(vmem_limit_bytes=8 << 20),
    )(*grads)


def solution(mesh):
    placed = (
        P("dp", ("outer", "inner"), None),
        P("dp", None),
        P("dp", ("outer", "inner")),
        P("dp", ("outer", "inner"), None),
    )
    return jax.shard_map(
        shards,
        mesh=mesh,
        in_specs=placed,
        out_specs=(P("dp", ("outer", "inner"), None), P("dp", None)),
        check_vma=False,
    )
```

time: 100 us -> 78 us (0.78)
  Pallas kernels: 95 us -> 77.2 us
  local copies, waits for them, and re-layouts: 4.38 us -> 0 us
    pallas_call x1 -> x2, Pallas kernels: 95 us -> 77.2 us  [the longest x1 75.4 us: shards(): pl.pallas_call(kernel, out_shape=(pltpu.VMEM((1, TOK, 4096), F32), pltpu....]
    unnamed x4 -> x0, local copies, waits for them, and re-layouts: 4.38 us -> none
where the time goes in v2:
time: 78 us; the launch traced here: 77.9 us
  Pallas kernels  77.2 us (99%)
    pallas_call x1, Pallas kernels, shards(): pl.pallas_call(kernel, out_shape=(pltpu.VMEM((1, TOK, 4096), F32), pltpu....  75.4 us
    pallas_call x1, Pallas kernels, shards(): pl.pallas_call(put, out_shape=(jax.ShapeDtypeStruct((1, TOK, 4096), F32),...  1.87 us

profile of v2, /device:TPU:1, one launch (start us, length us, event | category | flops | bytes accessed | tf_op | source)
XLA Modules:
  0.0 77.9 jit_solution(526692071871068859)
XLA Ops:
  0.6 75.4 %shard_map.68 = (f32[1,128,4096]{2,1,0:T(8,128)S(1)}, f32[1024,384]{1,0:T(8,128)S(1)}) custom-call(f32[1,128]{1,0:T(1,128)} %constant.2.clone.freq_hbm, bf16[1,128,4096]{2,1,0:T(8,128)(2,1)} %act_hbm.1, bf16[1024,384]{1,0:T(8,128)(2,1)} %w_hbm.1, s32[1,128]{1,0:T(1,128)} %pos_hbm.1, bf16[1,128,128]{2,1,0:T(8,128)(2,1)} %og_hbm.1), custom_call_target="tpu_custom_call" | custom-call | tf_op jit(solution)/shard_map/pallas_call | solution.py:546
  76.0 1.9 %shard_map.69 = (f32[1,128,4096]{2,1,0:T(8,128)}, f32[1024,384]{1,0:T(8,128)}) custom-call(f32[1,128,4096]{2,1,0:T(8,128)S(1)} %get-tuple-element.4.ga_ref, f32[1024,384]{1,0:T(8,128)S(1)} %get-tuple-element.5.gw_ref), custom_call_target="tpu_custom_call" | custom-call | tf_op jit(solution)/shard_map/pallas_call | solution.py:556

commit v3 on v2

--- a/solution.py
+++ b/solution.py
@@ -50,12 +50,13 @@
 
 def kernel(
     freq_hbm, act_hbm, w_hbm, pos_hbm, og_hbm, ga_ref, gw_ref,
-    freq_v, act_v, w_v, og_all, q_all, posq, posk, poskt, kv_all, kt_all, proj,
-    e_all, dp_all, ds_all, mb, lb, ab, dl, acc, p_all, st_all,
-    dq_out, dq_in, dkv_out, dkv_in, gp_all, actx, actxt,
+    freq_v, act_v, w_v, og_all, q_all, posq, posk, poskt, k_all, v_all, kt_all, proj,
+    e_all, dp_all, ds_all, mb, lb, ab, dl, acc_k, acc_v, p_all, st_all,
+    dq_out, dq_in, acc_own, dc_out, dc_in, dx_out, dx_in, gp_all, actx, actxt,
     dwx_out, dwx_in, mark, dwz_out, dwz_in, dw_all,
-    sent, lsem, wsem_y, wsem_x, wsem_c, psem, ksem, osem, qsem, kvsem_x, kvsem_c, asem, ssem,
-    dqsem, dkvsem, gsem_y, gsem_c, xsem, zsem, zgsem, xgsem, sgsem,
+    sent, lsem, wsem_y, wsem_x, wsem_c, psem, ksem, osem, qsem, kxsem, kcsem, vxsem, vcsem,
+    asem, ssem,
+    dqsem, dcsem, dxsem, gsem_y, gsem_c, xsem, zsem, zgsem, xgsem, sgsem,
 ):
     x, y, z, c = coords()
     other = 1 - c
@@ -113,8 +114,10 @@
         pl.semaphore_signal(barrier, inc=1, device_id=dev, device_id_type=MESH)
     pl.semaphore_wait(barrier, len(greet))
 
-    KVC, QC = pl.ds(HEAD_DIM, 2 * HEAD_DIM), pl.ds(0, HEAD_DIM)
-    COLS = (QC, KVC)
+    def third(i):
+        return pl.ds(i * HEAD_DIM, HEAD_DIM)
+
+    Q, K, V = range(3)
     YORDER = (1, 3, 2)
     odd = lax.rem(x, 2)
     near, far = odd * 2 + c, (1 - odd) * 2 + c
@@ -125,33 +128,33 @@
         return w_v.at[pl.ds(first_row, n), cols]
 
     def wshare(part, k):
-        owner, cols = lax.rem(y - k + NY, NY), COLS[part]
+        owner, cols = lax.rem(y - k + NY, NY), third(part)
         blk = wblock(owner, near, cols)
-        arrived(blk, wsem_y.at[part, k])
-        if part == 1 and k != 2:
+        arrived(blk, wsem_y.at[part, k - 1])
+        if part != Q and k != 2:
             half = wblock(owner, near, cols, 0 if k == 1 else 128, 128)
-            send(half, half, wsem_y.at[part, 2], ypeer(k))
+            send(half, half, wsem_y.at[part, 1], ypeer(k))
         for i, d in enumerate((1, 3)):
             half = wblock(owner, near, cols, i * 128, 128)
-            send(half, half, wsem_x.at[part, k], xpeer(d))
-        send(blk, blk, wsem_c.at[part, k], sibling)
+            send(half, half, wsem_x.at[part, k - 1], xpeer(d))
+        send(blk, blk, wsem_c.at[part, k - 1], sibling)
 
     def wpass(part, k):
-        owner, cols = lax.rem(y - k + NY, NY), COLS[part]
+        owner, cols = lax.rem(y - k + NY, NY), third(part)
         blk = wblock(owner, far, cols)
-        arrived(blk, wsem_x.at[part, k])
-        send(blk, blk, wsem_c.at[part, k], sibling)
+        arrived(blk, wsem_x.at[part, k - 1])
+        send(blk, blk, wsem_c.at[part, k - 1], sibling)
 
     def wuse(part, k):
-        owner, cols = lax.rem(y - k + NY, NY), COLS[part]
-        arrived(w_v.at[pl.ds(0, 512), cols], wsem_c.at[part, k])
+        owner, cols = lax.rem(y - k + NY, NY), third(part)
+        arrived(w_v.at[pl.ds(0, 512), cols], wsem_c.at[part, k - 1])
         proj[:, cols] += nn(acts(owner), w_v[rows(owner, 1024), cols])
 
     lw.wait()
-    for part in range(2):
+    for part in range(3):
         for k in (1, 3) if part else YORDER:
-            blk = wblock(y, near, COLS[part])
-            send(blk, blk, wsem_y.at[part, k], ypeer(k))
+            blk = wblock(y, near, third(part))
+            send(blk, blk, wsem_y.at[part, k - 1], ypeer(k))
     lo.wait()
     lp.wait()
     lk.wait()
@@ -177,35 +180,45 @@
         return act_v[:, pl.ds(pl.multiple_of(owner * 1024, 1024), 1024)]
 
     proj[...] = nn(acts(y), w_v[rows(y, 1024), :])
+    def along_x(blk, sem_x, sem_c):
+        for k in (2, 1, 3):
+            send(blk, blk, sem_x.at[k - 1], xpeer(k))
+        send(blk, blk, sem_c.at[0], sibling)
+
     for k in YORDER:
-        wshare(0, k)
-    wshare(1, 1)
-    wshare(1, 3)
+        wshare(Q, k)
+    wshare(K, 1)
+    wshare(K, 3)
+    wpass(Q, 1)
+    wpass(Q, 3)
+    wshare(V, 1)
+    wshare(V, 3)
+    wpass(Q, 2)
+    wshare(K, 2)
     for k in YORDER:
-        wpass(0, k)
-    for k in YORDER:
-        wuse(0, k)
-    queries = proj[:, :HEAD_DIM]
+        wuse(Q, k)
+    queries = proj[:, third(Q)]
     queries = queries * cosine + turn(queries) * sine
     q_all[rows(z, TOK), :] = queries.astype(BF)
     for k in range(1, NZ):
         blk = q_all.at[rows(z, TOK)]
         send(blk, blk, qsem, zpeer(k))
-    wshare(1, 2)
-    wpass(1, 1)
-    wpass(1, 3)
-    wuse(1, 1)
-    wuse(1, 3)
-    wpass(1, 2)
-    wuse(1, 2)
-    keys = proj[:, HEAD_DIM : 2 * HEAD_DIM]
+    wshare(V, 2)
+    for k in YORDER:
+        wpass(K, k)
+    wpass(V, 1)
+    wpass(V, 3)
+    for k in YORDER:
+        wuse(K, k)
+    keys = proj[:, third(K)]
     keys = keys * cosine + turn(keys) * sine
-    kv_all[xc, :, :HEAD_DIM] = keys.astype(BF)
-    kv_all[xc, :, HEAD_DIM:] = proj[:, 2 * HEAD_DIM :].astype(BF)
-    blk = kv_all.at[xc]
-    for k in (2, 1, 3):
-        send(blk, blk, kvsem_x.at[k], xpeer(k))
-    send(blk, blk, kvsem_c.at[0], sibling)
+    k_all[xc] = keys.astype(BF)
+    along_x(k_all.at[xc], kxsem, kcsem)
+    wpass(V, 2)
+    for k in YORDER:
+        wuse(V, k)
+    v_all[xc] = proj[:, third(V)].astype(BF)
+    along_x(v_all.at[xc], vxsem, vcsem)
 
     for k, d in cross:
         to_y, to_c = lax.rem(y + k, NY), c if d == 0 else other
@@ -220,42 +233,37 @@
     arrived(posk.at[pl.ds(0, 7)], ksem)
     for kb in range(8):
         poskt[kb] = jnp.broadcast_to(posk[kb].astype(F32), (TOK, TOK)).T
+    place_q = jnp.concatenate([posq[i].astype(F32) for i in range(NZ)], 1)
     arrived(og_all.at[pl.ds(0, 7 * TOK)], osem)
+
+    def block_of(step):
+        dx, dc = STEPS[step]
+        return lax.rem(x - dx + NX, NX) * 2 + (c if dc == 0 else other)
+
+    def relay(buf, sem_x, sem_c):
+        for k in (1, 3, 2):
+            blk = buf.at[lax.rem(x - k + NX, NX) * 2 + c]
+            arrived(blk, sem_x.at[k - 1])
+            send(blk, blk, sem_c.at[k], sibling)
+
+    relay(k_all, kxsem, kcsem)
+    relay(v_all, vxsem, vcsem)
     arrived(q_all.at[pl.ds(0, 7 * TOK)], qsem)
-    place_q = jnp.concatenate([posq[i].astype(F32) for i in range(NZ)], 1)
-
-    def step_of(j):
-        i = lax.rem(j + 1, 3)
-        dx = jnp.where(j < 2, 0, lax.rem(1 + 2 * i, 4) + i // 2)
-        return dx, jnp.where(j < 2, j, (j - 2) // 3)
-
-    def block_of(j):
-        dx, dc = step_of(j)
-        return lax.rem(x - dx + NX, NX) * 2 + lax.rem(c + dc, 2)
-
-    def relay(k):
-        blk = kv_all.at[lax.rem(x - k + NX, NX) * 2 + c]
-        arrived(blk, kvsem_x.at[k])
-        send(blk, blk, kvsem_c.at[k], sibling)
-
-    def first(k, carry, half):
-        kb = block_of(k)
-        dx, dc = step_of(k)
-        key = kv_all.at[kb, :, pl.ds(0, HEAD_DIM)]
-        value = kv_all.at[kb, :, pl.ds(HEAD_DIM, HEAD_DIM)]
+
+    def first(step, half):
+        kb = block_of(step)
+        dx, dc = STEPS[step]
         if half == 0:
-
-            @pl.when(dc > 0)
-            def _():
-                arrived(kv_all.at[kb], kvsem_c.at[dx])
-
-            kt_all[kb] = key[...].T
+            if dc:
+                arrived(k_all.at[kb], kcsem.at[dx])
+                arrived(v_all.at[kb], vcsem.at[dx])
+            kt_all[kb] = k_all[kb].T
         pk = poskt[kb]
         pk = jnp.concatenate([pk, pk], 1)
         for j in (2 * half, 2 * half + 1):
             cols = pl.ds(j * 256, 256)
-            s = nt(key[...], q_all[cols, :])
-            dp = nt(value[...], og_all[cols, :])
+            s = nt(k_all[kb], q_all[cols, :])
+            dp = nt(v_all[kb], og_all[cols, :])
             s = jnp.where(place_q[:, j * 256 : (j + 1) * 256] >= pk, s, LOW)
             top = jnp.max(s, 0, keepdims=True)
             e = jnp.exp2((s - top) * EXP2_SCALE)
@@ -264,13 +272,6 @@
             mb[pl.ds(kb, 1), cols] = top
             lb[pl.ds(kb, 1), cols] = jnp.sum(e, 0, keepdims=True)
             ab[pl.ds(kb, 1), cols] = jnp.sum(e * dp, 0, keepdims=True)
-        return carry
-
-    def first_half(k, carry):
-        return first(k, carry, 0)
-
-    def other_half(k, carry):
-        return first(k, carry, 1)
 
     def stats_send(half):
         cols = pl.ds(half * 512, 512)
@@ -321,60 +322,67 @@
                     device_id=device(x, y, to, c), device_id_type=MESH,
                 ).start()
 
-    lax.fori_loop(0, 2, first_half, 0, unroll=True)
-    relay(1)
-    relay(3)
-    lax.fori_loop(2, 4, first_half, 0, unroll=True)
-    relay(2)
-    lax.fori_loop(4, 8, first_half, 0, unroll=True)
+    for step in range(8):
+        first(step, 0)
     stats_send(0)
-    lax.fori_loop(0, 8, other_half, 0, unroll=True)
+    for step in range(8):
+        first(step, 1)
     stats_send(1)
     stats_merge(0)
 
-    def second_half0(k, carry):
+    for kb in range(8):
         dv = jnp.zeros((TOK, HEAD_DIM), F32)
         dk = jnp.zeros((TOK, HEAD_DIM), F32)
         for j in range(2):
             cols = pl.ds(j * 256, 256)
-            p, ds = grads_of(k, j)
+            p, ds = grads_of(kb, j)
             dv += nn(p, og_all[cols, :])
             dk += nn(ds, q_all[cols, :])
-        acc[k, :, :HEAD_DIM] = dk
-        acc[k, :, HEAD_DIM:] = dv
-        return carry
-
-    lax.fori_loop(0, 8, second_half0, 0, unroll=True)
+        acc_k[kb] = dk
+        acc_v[kb] = dv
     dq_send(0)
     stats_merge(1)
-
-    def second_half1(k, carry):
+    for kb in range(8):
         for j in range(2, 4):
-            p, ds = grads_of(k, j)
-            p_all[k, :, pl.ds((j - 2) * 256, 256)] = p
-        return carry
-
-    lax.fori_loop(0, 8, second_half1, 0, unroll=True)
+            p, ds = grads_of(kb, j)
+            p_all[kb, :, pl.ds((j - 2) * 256, 256)] = p
     dq_send(1)
 
-    def key_grads(i, carry):
-        k = 7 - i
-        kb = block_of(k)
-        dk = acc[kb, :, :HEAD_DIM] + nn(ds_all[rows(kb, TOK), 512:], q_all[512:, :])
-        dv = acc[kb, :, HEAD_DIM:] + nn(p_all[kb], og_all[512:, :])
-        dkv_out[kb, :, :HEAD_DIM] = (dk * SCALE).astype(BF)
-        dkv_out[kb, :, HEAD_DIM:] = dv.astype(BF)
-
-        @pl.when(k > 0)
-        def _():
-            pltpu.make_async_remote_copy(
-                dkv_out.at[kb], dkv_in.at[xc], sent, dkvsem,
-                device_id=device(kb // 2, y, z, lax.rem(kb, 2)), device_id_type=MESH,
-            ).start()
-
-        return carry
-
-    lax.fori_loop(0, 8, key_grads, 0, unroll=True)
+    XORDER = (2, 1, 3, 0)
+
+    def value_grad(kb):
+        return acc_v[kb] + nn(p_all[kb], og_all[512:, :])
+
+    def key_grad(kb):
+        return (acc_k[kb] + nn(ds_all[rows(kb, TOK), 512:], q_all[512:, :])) * SCALE
+
+    def to_sibling(i, grad):
+        for k in XORDER:
+            dc_out[i, k] = grad(lax.rem(x + k, NX) * 2 + other).astype(BF)
+        send(dc_out.at[i], dc_in.at[i], dcsem.at[i], sibling)
+
+    def to_owners(i, own):
+        arrived(dc_in.at[i], dcsem.at[i])
+        for k in XORDER:
+            dx_out[i, k] = (own[k] + dc_in[i, k].astype(F32)).astype(BF)
+        for k in XORDER[:3]:
+            send(dx_out.at[i, k], dx_in.at[i, k], dxsem.at[i], xpeer(k))
+
+    def collect(i):
+        arrived(dx_in.at[i, pl.ds(1, 3)], dxsem.at[i])
+        total = dx_out[i, 0].astype(F32)
+        for k in range(1, NX):
+            total += dx_in[i, k].astype(F32)
+        return total
+
+    to_sibling(0, value_grad)
+    to_sibling(1, key_grad)
+    for k in XORDER:
+        acc_own[0, k] = value_grad(lax.rem(x + k, NX) * 2 + c)
+    for k in XORDER:
+        acc_own[1, k] = key_grad(lax.rem(x + k, NX) * 2 + c)
+    to_owners(0, acc_own.at[0])
+    to_owners(1, acc_own.at[1])
     lx.wait()
     arrived(actx.at[pl.ds(0, 7)], asem)
 
@@ -383,28 +391,16 @@
         return carry
 
     lax.fori_loop(0, 8, turn_block, 0)
-    arrived(dkv_in.at[pl.ds(0, 7)], dkvsem)
-    dkv = dkv_out[xc].astype(F32)
-    for k in range(1, 8):
-        dkv += dkv_in[lax.rem(xc + k, 8)].astype(F32)
-    dkey = dkv[:, :HEAD_DIM]
-    dkey = dkey * cosine - turn(dkey) * sine
-    gp_all[yc, :, HEAD_DIM : 2 * HEAD_DIM] = dkey.astype(BF)
-    gp_all[yc, :, 2 * HEAD_DIM :] = dkv[:, HEAD_DIM:].astype(BF)
-
-    def third(i):
-        return pl.ds(i * HEAD_DIM, HEAD_DIM)
-
     def gp_send(i):
         blk = gp_all.at[yc, :, third(i)]
         for k in (2, 1, 3):
-            send(blk, blk, gsem_y.at[i, k], ypeer(k))
+            send(blk, blk, gsem_y.at[i, k - 1], ypeer(k))
         send(blk, blk, gsem_c.at[i], sibling)
 
     def gp_relay(i):
         for k in YORDER:
             blk = gp_all.at[lax.rem(y - k + NY, NY) * 2 + c, :, third(i)]
-            arrived(blk, gsem_y.at[i, k])
+            arrived(blk, gsem_y.at[i, k - 1])
             send(blk, blk, gsem_c.at[i], sibling)
 
     def dw_send(i):
@@ -444,20 +440,24 @@
         arrived(dw_all.at[i, pl.ds(0, 7 * 16)], zgsem.at[i])
         blk = band(i, x, c)
         for k in (2, 1, 3):
-            send(blk, blk, xgsem.at[i, k], xpeer(k))
+            send(blk, blk, xgsem.at[i, k - 1], xpeer(k))
         send(blk, blk, sgsem.at[i], sibling)
 
     def spread_relay(i):
         for k in (1, 3, 2):
             blk = band(i, lax.rem(x - k + NX, NX), c)
-            arrived(blk, xgsem.at[i, k])
+            arrived(blk, xgsem.at[i, k - 1])
             send(blk, blk, sgsem.at[i], sibling)
 
     def finish(i):
         arrived(dw_all.at[i, pl.ds(0, 512)], sgsem.at[i])
         gw_ref[:, third(i)] = dw_all[i].astype(F32)
 
+    gp_all[yc, :, third(2)] = collect(0).astype(BF)
     gp_send(2)
+    dkey = collect(1)
+    dkey = dkey * cosine - turn(dkey) * sine
+    gp_all[yc, :, third(1)] = dkey.astype(BF)
     gp_send(1)
     arrived(dq_in.at[pl.ds(0, 7)], dqsem)
     dq = dq_out[z].astype(F32)
@@ -473,7 +473,7 @@
         ga_ref[0, :, cols] = nt(gp_all[yc], w_v[cols, :])
         return carry
 
-    lax.fori_loop(0, 8, acts_grad, 0)
+    lax.fori_loop(0, 6, acts_grad, 0)
     gp_relay(2)
     dw_send(2)
     gp_relay(1)
@@ -484,6 +484,7 @@
     band_send(1)
     band_send(0)
     piece_send(2)
+    lax.fori_loop(6, 8, acts_grad, 0)
     piece_send(1)
     piece_send(0)
     spread(2)
@@ -496,11 +497,10 @@
     finish(1)
     finish(0)
 
-    for out, sem in ((dkv_out, dkvsem), (dq_out, dqsem)):
-        blk = out.at[pl.ds(0, 7)]
-        pltpu.make_async_remote_copy(
-            blk, blk, sent, sem, device_id=sibling, device_id_type=MESH
-        ).wait_send()
+    blk = dq_out.at[pl.ds(0, 7)]
+    pltpu.make_async_remote_copy(
+        blk, blk, sent, dqsem, device_id=sibling, device_id_type=MESH
+    ).wait_send()
     for cp in sends:
         cp.wait_send()
 
@@ -530,18 +530,19 @@
     scratch = [
         V((1, HEAD_DIM), F32), V((TOK, 4096), BF), V((4096, WIDE), BF), V((1024, HEAD_DIM), BF), V((1024, HEAD_DIM), BF),
         V((NZ, 1, TOK), jnp.int32), V((8, 1, TOK), jnp.int32), V((8, TOK, TOK), F32),
-        V((8, TOK, 2 * HEAD_DIM), BF), V((8, HEAD_DIM, TOK), BF), V((TOK, WIDE), F32),
+        V((8, TOK, HEAD_DIM), BF), V((8, TOK, HEAD_DIM), BF), V((8, HEAD_DIM, TOK), BF), V((TOK, WIDE), F32),
         V((8, TOK, 1024), F32), V((8, TOK, 1024), F32), V((1024, 1024), BF),
         V((8, 1024), F32), V((8, 1024), F32), V((8, 1024), F32), V((1, 1024), F32),
-        V((8, TOK, 2 * HEAD_DIM), F32), V((8, TOK, 512), BF), V((2, NZ, 2, 512), F32),
+        V((8, TOK, HEAD_DIM), F32), V((8, TOK, HEAD_DIM), F32), V((8, TOK, 512), BF), V((2, NZ, 2, 512), F32),
         V((NZ, HEAD_DIM, TOK), BF), V((NZ, HEAD_DIM, TOK), BF),
-        V((8, TOK, 2 * HEAD_DIM), BF), V((8, TOK, 2 * HEAD_DIM), BF),
+        V((2, NX, TOK, HEAD_DIM), F32), V((2, NX, TOK, HEAD_DIM), BF), V((2, NX, TOK, HEAD_DIM), BF),
+        V((2, NX, TOK, HEAD_DIM), BF), V((2, NX, TOK, HEAD_DIM), BF),
         V((8, TOK, WIDE), BF), V((8, TOK, 512), BF), V((512, 1024), BF),
         V((3, NX, 128, 128), BF), V((3, NX, 128, 128), BF), V((8, 128), F32),
         V((3, NZ, 16, 128), BF), V((3, NZ, 16, 128), BF), V((3, 1024, 128), BF),
-        dma(()), dma((4,)), dma((2, 4)), dma((2, 4)), dma((2, 4)), dma(()), dma(()), dma(()), dma(()),
-        dma((4,)), dma((4,)), dma(()), dma((2,)), dma(()), dma(()), dma((3, 4)), dma((3,)), dma((3,)),
-        dma((3,)), dma((3,)), dma((3, 4)), dma((3,)),
+        dma(()), dma((4,)), dma((3, 3)), dma((3, 3)), dma((3, 3)), dma(()), dma(()), dma(()), dma(()),
+        dma((3,)), dma((4,)), dma((3,)), dma((4,)), dma(()), dma((2,)), dma(()), dma((2,)), dma((2,)), dma((3, 3)), dma((3,)), dma((3,)),
+        dma((3,)), dma((3,)), dma((3, 3)), dma((3,)),
     ]
     grads = pl.pallas_call(
         kernel,

time: 78 us -> 76.1 us (0.976)
  Pallas kernels: 77.2 us -> 75.3 us
    pallas_call x1, Pallas kernels: 75.4 us -> 73.5 us  [shards(): pl.pallas_call(kernel, out_shape=(pltpu.VMEM((1, TOK, 4096), F32), pltpu....]
where the time goes in v3:
time: 76.1 us; the launch traced here: 76 us
  Pallas kernels  75.3 us (99%)
    pallas_call x1, Pallas kernels, shards(): pl.pallas_call(kernel, out_shape=(pltpu.VMEM((1, TOK, 4096), F32), pltpu....  73.5 us
    pallas_call x1, Pallas kernels, shards(): pl.pallas_call(put, out_shape=(jax.ShapeDtypeStruct((1, TOK, 4096), F32),...  1.87 us

profile of v3, /device:TPU:1, one launch (start us, length us, event | category | flops | bytes accessed | tf_op | source)
XLA Modules:
  0.0 76.0 jit_solution(17450785531211510779)
XLA Ops:
  0.6 73.5 %shard_map.68 = (f32[1,128,4096]{2,1,0:T(8,128)S(1)}, f32[1024,384]{1,0:T(8,128)S(1)}) custom-call(f32[1,128]{1,0:T(1,128)} %constant.2.clone.freq_hbm, bf16[1,128,4096]{2,1,0:T(8,128)(2,1)} %act_hbm.1, bf16[1024,384]{1,0:T(8,128)(2,1)} %w_hbm.1, s32[1,128]{1,0:T(1,128)} %pos_hbm.1, bf16[1,128,128]{2,1,0:T(8,128)(2,1)} %og_hbm.1), custom_call_target="tpu_custom_call" | custom-call | tf_op jit(solution)/shard_map/pallas_call | solution.py:547
  74.1 1.9 %shard_map.69 = (f32[1,128,4096]{2,1,0:T(8,128)}, f32[1024,384]{1,0:T(8,128)}) custom-call(f32[1,128,4096]{2,1,0:T(8,128)S(1)} %get-tuple-element.4.ga_ref, f32[1024,384]{1,0:T(8,128)S(1)} %get-tuple-element.5.gw_ref), custom_call_target="tpu_custom_call" | custom-call | tf_op jit(solution)/shard_map/pallas_call | solution.py:557

commit v4 on v3

--- a/solution.py
+++ b/solution.py
@@ -54,7 +54,7 @@
     e_all, dp_all, ds_all, mb, lb, ab, dl, acc_k, acc_v, p_all, st_all,
     dq_out, dq_in, acc_own, dc_out, dc_in, dx_out, dx_in, gp_all, actx, actxt,
     dwx_out, dwx_in, mark, dwz_out, dwz_in, dw_all,
-    sent, lsem, wsem_y, wsem_x, wsem_c, psem, ksem, osem, qsem, kxsem, kcsem, vxsem, vcsem,
+    word, sent, lsem, wsem_y, wsem_x, wsem_c, psem, ksem, osem, qsem, kxsem, kcsem, vxsem, vcsem,
     asem, ssem,
     dqsem, dcsem, dxsem, gsem_y, gsem_c, xsem, zsem, zgsem, xgsem, sgsem,
 ):
@@ -103,7 +103,7 @@
     lf.start()
 
     barrier = pltpu.get_barrier_semaphore()
-    greet = [sibling] + [zpeer(k) for k in range(1, NZ)]
+    greet = [sibling, zpeer(1), zpeer(NZ - 1)]
     for k in range(1, 4):
         greet += [xpeer(k), ypeer(k)]
         greet += [
@@ -155,10 +155,39 @@
         for k in (1, 3) if part else YORDER:
             blk = wblock(y, near, third(part))
             send(blk, blk, wsem_y.at[part, k - 1], ypeer(k))
+    def word_send(r):
+        for k in (1, NZ - 1):
+            pl.semaphore_signal(word.at[r], inc=1, device_id=zpeer(k), device_id_type=MESH)
+
+    word_send(0)
     lo.wait()
     lp.wait()
     lk.wait()
     lf.wait()
+    place = posq[z].astype(F32)
+    angles = jnp.broadcast_to(place, (TOK, HEAD_DIM)).T * freq_v[...]
+    cosine, sine = jnp.cos(angles), jnp.sin(angles)
+
+    la.wait()
+
+    def acts(owner):
+        return act_v[:, pl.ds(pl.multiple_of(owner * 1024, 1024), 1024)]
+
+    proj[...] = nn(acts(y), w_v[rows(y, 1024), :])
+    def along_x(blk, sem_x, sem_c):
+        for k in (2, 1, 3):
+            send(blk, blk, sem_x.at[k - 1], xpeer(k))
+        send(blk, blk, sem_c.at[0], sibling)
+
+    pl.semaphore_wait(word.at[0], 2)
+    word_send(1)
+    for k in YORDER:
+        wshare(Q, k)
+    pl.semaphore_wait(word.at[1], 2)
+    word_send(2)
+    wshare(K, 1)
+    wshare(K, 3)
+    pl.semaphore_wait(word.at[2], 2)
     for k in range(1, NZ):
         blk = posq.at[z]
         send(blk, blk, psem, zpeer(k))
@@ -169,26 +198,6 @@
     for k in range(1, NZ):
         blk = og_all.at[rows(z, TOK)]
         send(blk, blk, osem, zpeer(k))
-
-    place = posq[z].astype(F32)
-    angles = jnp.broadcast_to(place, (TOK, HEAD_DIM)).T * freq_v[...]
-    cosine, sine = jnp.cos(angles), jnp.sin(angles)
-
-    la.wait()
-
-    def acts(owner):
-        return act_v[:, pl.ds(pl.multiple_of(owner * 1024, 1024), 1024)]
-
-    proj[...] = nn(acts(y), w_v[rows(y, 1024), :])
-    def along_x(blk, sem_x, sem_c):
-        for k in (2, 1, 3):
-            send(blk, blk, sem_x.at[k - 1], xpeer(k))
-        send(blk, blk, sem_c.at[0], sibling)
-
-    for k in YORDER:
-        wshare(Q, k)
-    wshare(K, 1)
-    wshare(K, 3)
     wpass(Q, 1)
     wpass(Q, 3)
     wshare(V, 1)
@@ -473,18 +482,19 @@
         ga_ref[0, :, cols] = nt(gp_all[yc], w_v[cols, :])
         return carry
 
-    lax.fori_loop(0, 6, acts_grad, 0)
+    lax.fori_loop(0, 3, acts_grad, 0)
     gp_relay(2)
+    lax.fori_loop(3, 5, acts_grad, 0)
+    gp_relay(1)
     dw_send(2)
-    gp_relay(1)
+    gp_relay(0)
     dw_send(1)
-    gp_relay(0)
     dw_send(0)
     band_send(2)
     band_send(1)
     band_send(0)
     piece_send(2)
-    lax.fori_loop(6, 8, acts_grad, 0)
+    lax.fori_loop(5, 8, acts_grad, 0)
     piece_send(1)
     piece_send(0)
     spread(2)
@@ -540,7 +550,7 @@
         V((8, TOK, WIDE), BF), V((8, TOK, 512), BF), V((512, 1024), BF),
         V((3, NX, 128, 128), BF), V((3, NX, 128, 128), BF), V((8, 128), F32),
         V((3, NZ, 16, 128), BF), V((3, NZ, 16, 128), BF), V((3, 1024, 128), BF),
-        dma(()), dma((4,)), dma((3, 3)), dma((3, 3)), dma((3, 3)), dma(()), dma(()), dma(()), dma(()),
+        pltpu.SemaphoreType.REGULAR((3,)), dma(()), dma((4,)), dma((3, 3)), dma((3, 3)), dma((3, 3)), dma(()), dma(()), dma(()), dma(()),
         dma((3,)), dma((4,)), dma((3,)), dma((4,)), dma(()), dma((2,)), dma(()), dma((2,)), dma((2,)), dma((3, 3)), dma((3,)), dma((3,)),
         dma((3,)), dma((3,)), dma((3, 3)), dma((3,)),
     ]

time: 76.1 us -> 76.1 us (level)
  no operation moved by 1% of the time
where the time goes in v4:
time: 76.1 us; the launch traced here: 76 us
  Pallas kernels  75.4 us (99%)
    pallas_call x1, Pallas kernels, shards(): pl.pallas_call(kernel, out_shape=(pltpu.VMEM((1, TOK, 4096), F32), pltpu....  73.5 us
    pallas_call x1, Pallas kernels, shards(): pl.pallas_call(put, out_shape=(jax.ShapeDtypeStruct((1, TOK, 4096), F32),...  1.87 us

profile of v4, /device:TPU:1, one launch (start us, length us, event | category | flops | bytes accessed | tf_op | source)
XLA Modules:
  0.0 76.0 jit_solution(14337691600754621364)
XLA Ops:
  0.6 73.5 %shard_map.68 = (f32[1,128,4096]{2,1,0:T(8,128)S(1)}, f32[1024,384]{1,0:T(8,128)S(1)}) custom-call(f32[1,128]{1,0:T(1,128)} %constant.2.clone.freq_hbm, bf16[1,128,4096]{2,1,0:T(8,128)(2,1)} %act_hbm.1, bf16[1024,384]{1,0:T(8,128)(2,1)} %w_hbm.1, s32[1,128]{1,0:T(1,128)} %pos_hbm.1, bf16[1,128,128]{2,1,0:T(8,128)(2,1)} %og_hbm.1), custom_call_target="tpu_custom_call" | custom-call | tf_op jit(solution)/shard_map/pallas_call | solution.py:557
  74.2 1.9 %shard_map.69 = (f32[1,128,4096]{2,1,0:T(8,128)}, f32[1024,384]{1,0:T(8,128)}) custom-call(f32[1,128,4096]{2,1,0:T(8,128)S(1)} %get-tuple-element.4.ga_ref, f32[1024,384]{1,0:T(8,128)S(1)} %get-tuple-element.5.gw_ref), custom_call_target="tpu_custom_call" | custom-call | tf_op jit(solution)/shard_map/pallas_call | solution.py:567

commit v5 on v4

--- a/solution.py
+++ b/solution.py
@@ -209,7 +209,7 @@
     queries = proj[:, third(Q)]
     queries = queries * cosine + turn(queries) * sine
     q_all[rows(z, TOK), :] = queries.astype(BF)
-    for k in range(1, NZ):
+    for k in (4, 3, 5, 2, 6, 1, 7):
         blk = q_all.at[rows(z, TOK)]
         send(blk, blk, qsem, zpeer(k))
     wshare(V, 2)
@@ -291,7 +291,7 @@
         st_all[half, z, 0:1, :] = top * EXP2_SCALE + jnp.log2(total)
         st_all[half, z, 1:2, :] = jnp.sum(ab[:, cols] * fade, 0, keepdims=True) / total
         blk = st_all.at[half, z]
-        for k in range(1, NZ):
+        for k in (4, 3, 5, 2, 6, 1, 7):
             send(blk, blk, ssem.at[half], zpeer(k))
 
     def stats_merge(half):
@@ -322,13 +322,14 @@
             dq = nn(kt, ds_all[:, j * 256 : (j + 1) * 256]) * SCALE
             dq_out[2 * j] = dq[:, :TOK].astype(BF)
             dq_out[2 * j + 1] = dq[:, TOK:].astype(BF)
-        for to in range(4 * half, 4 * half + 4):
-
-            @pl.when(z != to)
+        for k in (4, 3, 5, 2, 6, 1, 7):
+            to = lax.rem(z + k, NZ)
+
+            @pl.when(to // 4 == half)
             def _():
                 pltpu.make_async_remote_copy(
                     dq_out.at[to], dq_in.at[z], sent, dqsem,
-                    device_id=device(x, y, to, c), device_id_type=MESH,
+                    device_id=zpeer(k), device_id_type=MESH,
                 ).start()
 
     for step in range(8):

time: 76.1 us -> 76 us (level)
  no operation moved by 1% of the time
where the time goes in v5:
time: 76 us; the launch traced here: 75.9 us
  Pallas kernels  75.3 us (99%)
    pallas_call x1, Pallas kernels, shards(): pl.pallas_call(kernel, out_shape=(pltpu.VMEM((1, TOK, 4096), F32), pltpu....  73.4 us
    pallas_call x1, Pallas kernels, shards(): pl.pallas_call(put, out_shape=(jax.ShapeDtypeStruct((1, TOK, 4096), F32),...  1.87 us

profile of v5, /device:TPU:1, one launch (start us, length us, event | category | flops | bytes accessed | tf_op | source)
XLA Modules:
  0.0 75.9 jit_solution(10294043623023823453)
XLA Ops:
  0.6 73.4 %shard_map.68 = (f32[1,128,4096]{2,1,0:T(8,128)S(1)}, f32[1024,384]{1,0:T(8,128)S(1)}) custom-call(f32[1,128]{1,0:T(1,128)} %constant.2.clone.freq_hbm, bf16[1,128,4096]{2,1,0:T(8,128)(2,1)} %act_hbm.1, bf16[1024,384]{1,0:T(8,128)(2,1)} %w_hbm.1, s32[1,128]{1,0:T(1,128)} %pos_hbm.1, bf16[1,128,128]{2,1,0:T(8,128)(2,1)} %og_hbm.1), custom_call_target="tpu_custom_call" | custom-call | tf_op jit(solution)/shard_map/pallas_call | solution.py:558
  74.1 1.9 %shard_map.69 = (f32[1,128,4096]{2,1,0:T(8,128)}, f32[1024,384]{1,0:T(8,128)}) custom-call(f32[1,128,4096]{2,1,0:T(8,128)S(1)} %get-tuple-element.4.ga_ref, f32[1024,384]{1,0:T(8,128)S(1)} %get-tuple-element.5.gw_ref), custom_call_target="tpu_custom_call" | custom-call | tf_op jit(solution)/shard_map/pallas_call | solution.py:568

commit v6 on v5

--- a/solution.py
+++ b/solution.py
@@ -152,7 +152,7 @@
 
     lw.wait()
     for part in range(3):
-        for k in (1, 3) if part else YORDER:
+        for k in (1, 3) if part else (2, 1, 3):
             blk = wblock(y, near, third(part))
             send(blk, blk, wsem_y.at[part, k - 1], ypeer(k))
     def word_send(r):

time: 76 us -> 75.7 us (level)
  no operation moved by 1% of the time
where the time goes in v6:
time: 75.7 us; the launch traced here: 75.6 us
  Pallas kernels  75 us (99%)
    pallas_call x1, Pallas kernels, shards(): pl.pallas_call(kernel, out_shape=(pltpu.VMEM((1, TOK, 4096), F32), pltpu....  73.1 us
    pallas_call x1, Pallas kernels, shards(): pl.pallas_call(put, out_shape=(jax.ShapeDtypeStruct((1, TOK, 4096), F32),...  1.87 us

profile of v6, /device:TPU:1, one launch (start us, length us, event | category | flops | bytes accessed | tf_op | source)
XLA Modules:
  0.0 75.6 jit_solution(1090227480673600758)
XLA Ops:
  0.6 73.1 %shard_map.68 = (f32[1,128,4096]{2,1,0:T(8,128)S(1)}, f32[1024,384]{1,0:T(8,128)S(1)}) custom-call(f32[1,128]{1,0:T(1,128)} %constant.2.clone.freq_hbm, bf16[1,128,4096]{2,1,0:T(8,128)(2,1)} %act_hbm.1, bf16[1024,384]{1,0:T(8,128)(2,1)} %w_hbm.1, s32[1,128]{1,0:T(1,128)} %pos_hbm.1, bf16[1,128,128]{2,1,0:T(8,128)(2,1)} %og_hbm.1), custom_call_target="tpu_custom_call" | custom-call | tf_op jit(solution)/shard_map/pallas_call | solution.py:558
  73.8 1.9 %shard_map.69 = (f32[1,128,4096]{2,1,0:T(8,128)}, f32[1024,384]{1,0:T(8,128)}) custom-call(f32[1,128,4096]{2,1,0:T(8,128)S(1)} %get-tuple-element.4.ga_ref, f32[1024,384]{1,0:T(8,128)S(1)} %get-tuple-element.5.gw_ref), custom_call_target="tpu_custom_call" | custom-call | tf_op jit(solution)/shard_map/pallas_call | solution.py:568
